TPU v7x, 256 devices: a whole 4x4x8 slice. The times are simulated.
256 devices in a mesh: rows: 256 (over y, z, x, core).
Axes of the slice: x: 4, y: 4, z: 8, core: 2. Of those that a mesh axis runs over, the one named last changes fastest.
Arguments:
- right_side: float32 [4194304], P('rows'), may hold values from -24 to 24
- diag_shift: float32 [4194304], P('rows'), may hold values from 0.05 to 0.5
- dictionary: float32 [128, 128, 128], replicated, may hold values from -16.5 to 16.5, as said below
- diag_ids: int32 [32768], P('rows'), may hold values from 0 to 127
- diag_gain: float32 [32768], P('rows'), may hold values from 0.3 to 1.5
- cycle_ids: int32 [32768, 2], P('rows'), may hold values from 0 to 127, as said below
- cycle_weights: float32 [32768, 2], P('rows'), may hold values from 0.3 to 1.5, as said below
- link_rows: int32 [256, 5, 64], P('rows'), may hold values from 0 to 127, as said below
- link_ids: int32 [256, 5, 64], P('rows'), may hold values from 0 to 127, as said below
- link_weights: float32 [256, 5, 64], P('rows'), may hold values from 0.3 to 1.5, as said below
Outputs:
- solution_field: float32 [4194304], P('rows')
- residual: float32 [4194304], P('rows')
Inputs may be any that keep to these rules, and one draw needn't show every extreme that they name: `dictionary`: every block is symmetric positive definite. cycle_ids[i,1] equals cycle_ids[(i+1) mod 32768,0]. cycle_weights[i,1] equals cycle_weights[(i+1) mod 32768,0]. `link_rows`: for each device and level the 64 entries are distinct. `link_ids`: devices d and d XOR 2^b at level m (b = log2 of the number of devices - 1 - m) hold the same entries in the same order. `link_weights`: devices d and d XOR 2^b at level m (b = log2 of the number of devices - 1 - m) hold the same entries in the same order.
All inputs are finite; a program needn't handle non-finite values.
Results may differ from a plain program's by a relative error of at most 0.0003.
Values sent between devices are 32-bit elements; how exact they have to be, the bound alone decides.
A program may use at most 128 MiB of HBM per device.

v0:
```python
import jax
import jax.numpy as jnp
from jax import lax
from jax.sharding import Mesh
from jax.sharding import PartitionSpec as P

ITERS = 4
ROWS = ("rows_0", "rows_1", "rows_2", "rows_3")


def extended(array, sides, width):
    for axis, dim in sides:
        count, length = (lax.axis_size(axis), array.shape[dim])
        up = [(i, (i + 1) % count) for i in range(count)]
        down = [(j, i) for i, j in up]
        last = lax.slice_in_dim(array, length - width, length, axis=dim)
        first = lax.slice_in_dim(array, 0, width, axis=dim)
        before = lax.ppermute(last, axis, up)
        after = lax.ppermute(first, axis, down)
        array = jnp.concatenate([before, array, after], axis=dim)
    return array


def from_partner(value, axis, stride):
    mask = 2**stride
    pairs = [(source, source ^ mask) for source in range(lax.axis_size(axis))]
    return lax.ppermute(value, axis, pairs)


def one_axis_at_a_time(array, axes):
    for axis in axes:
        array = lax.psum(array, axis)
    return array


def batched(mats, vectors):
    return jnp.einsum("nij,nj->ni", mats, vectors, precision=lax.Precision.HIGHEST)


def per_device(
    right_side,
    diag_shift,
    dictionary,
    diag_ids,
    diag_gain,
    cycle_ids,
    cycle_weights,
    link_rows,
    link_ids,
    link_weights,
):
    blocks = diag_ids.shape[0]
    block_width = dictionary.shape[1]
    bit_count = lax.axis_size(ROWS).bit_length() - 1
    levels = link_rows.shape[1]
    own_rows = link_rows[0]
    shifts = diag_shift.reshape(blocks, block_width)
    diag_mats = dictionary[diag_ids] * diag_gain[:, None, None]
    edge_mats = dictionary[cycle_ids[:, 0]] * cycle_weights[:, 0, None, None]
    last_edge = dictionary[cycle_ids[-1, 1]] * cycle_weights[-1, 1]
    link_mats = dictionary[link_ids[0]] * link_weights[0][:, :, None, None]
    selector = (own_rows[:, :, None] == jnp.arange(blocks, dtype=jnp.int32)).astype(jnp.float32)

    def operate(vector):
        block_vec = vector.reshape(blocks, block_width)
        padded = extended(block_vec, ((ROWS, 0),), 1)
        result = shifts * block_vec + batched(diag_mats, block_vec)
        flux = batched(edge_mats, block_vec - padded[:-2])
        tail = jnp.dot(last_edge, padded[-1] - block_vec[-1], precision=lax.Precision.HIGHEST)
        next_flux = jnp.concatenate([flux[1:], tail[None]], axis=0)
        result = result + flux - next_flux
        differences = []
        for level_idx in range(levels):
            swap_bit = bit_count - 1 - level_idx
            own_part = block_vec[own_rows[level_idx]]
            remote = from_partner(own_part, ROWS, swap_bit)
            differences.append(own_part - remote)
        products = jnp.einsum(
            "lhij,lhj->lhi", link_mats, jnp.stack(differences), precision=lax.Precision.HIGHEST
        )
        result = result + jnp.einsum(
            "lhn,lhi->ni", selector, products, precision=lax.Precision.HIGHEST
        )
        return result.reshape(-1)

    def inner_sums(residual, image_vec):
        return (
            one_axis_at_a_time(jnp.sum(residual * residual), ROWS),
            one_axis_at_a_time(jnp.sum(residual * image_vec), ROWS),
        )

    solution_field = jnp.zeros_like(right_side)
    residual = right_side
    image_vec = operate(residual)
    norm_now, product = inner_sums(residual, image_vec)
    step_size = norm_now / product
    direction, image_dir = (residual, image_vec)
    for iteration in range(ITERS):
        solution_field = solution_field + step_size * direction
        residual = residual - step_size * image_dir
        if iteration + 1 < ITERS:
            image_vec = operate(residual)
            norm_next, product = inner_sums(residual, image_vec)
            beta_ratio = norm_next / norm_now
            step_size = norm_next / (product - beta_ratio * norm_next / step_size)
            direction = residual + beta_ratio * direction
            image_dir = image_vec + beta_ratio * image_dir
            norm_now = norm_next
    return (solution_field, residual)


def solution(mesh):
    torus = Mesh(mesh.devices.reshape(4, 8, 4, 2), ("rows_0", "rows_1", "rows_2", "rows_3"))
    placed = (
        P(ROWS),
        P(ROWS),
        P(),
        P(ROWS),
        P(ROWS),
        P(ROWS, None),
        P(ROWS, None),
        P(ROWS, None, None),
        P(ROWS, None, None),
        P(ROWS, None, None),
    )
    return jax.shard_map(
        per_device, mesh=torus, in_specs=placed, out_specs=(P(ROWS), P(ROWS)), check_vma=False
    )
```

profile of v0, /device:TPU:1, one launch (start us, length us, event | category | flops | bytes accessed | tf_op | source)
XLA Modules:
  0.0 564.1 jit_solution(6718864532662220363)
XLA Ops:
  38.7 15.5 %fusion.26 = f32[128,1,128]{2,1,0:T(1,128)S(1)} fusion(f32[128,128,1]{1,2,0:T(1,128)S(1)} %bitcast.304, f32[128,128,128]{2,1,0:T(8,128)} %gather_fusion, f32[128]{0:T(128)S(1)} %copy-done.2), kind=kOutput, calls=%fused_computation.49 | convolution fusion | flops 27262976 | bytes 8520192 | tf_op jit(solution)/shard_map/nij,nj->ni/dot_general | solution.py:37
  54.2 17.2 %gather_fusion.2 = f32[320,128,128]{2,1,0:T(8,128)} fusion(f32[128,128,128]{2,1,0:T(8,128)} %param.12, s32[1024]{0:T(1024)S(1)} %get-tuple-element.63), kind=kCustom, calls=%fused_computation.2 | custom fusion | bytes 41944320 | tf_op jit(solution)/shard_map/gather | solution.py:61
  81.7 15.5 %fusion.18 = f32[128,1,128]{2,1,0:T(1,128)S(1)} fusion(f32[128,128,1]{1,2,0:T(1,128)S(1)} %bitcast.338, f32[128,128,128]{2,1,0:T(8,128)} %gather_fusion.1, f32[128]{0:T(128)S(1)} %slice_bitcast_fusion.8), kind=kOutput, calls=%fused_computation.41 | convolution fusion | flops 27262976 | bytes 8520192 | tf_op jit(solution)/shard_map/nij,nj->ni/dot_general | solution.py:37
  100.1 35.7 %fusion.6 = f32[5,64,1,128]{3,2,1,0:T(1,128)S(1)} fusion(f32[5,64,128,1]{2,3,1,0:T(1,128)S(1)} %bitcast.329, f32[5,64,128,128]{3,2,1,0:T(8,128)} %bitcast.281, f32[5,64]{1,0:T(8,128)S(1)} %bitcast.313), kind=kOutput, calls=%fused_computation.29 | convolution fusion | flops 68157440 | bytes 21300480 | tf_op jit(solution)/shard_map/lhij,lhj->lhi/dot_general | solution.py:78
  144.5 12.3 %all-reduce.3 = (f32[]{:T(128)}, f32[]{:T(128)}) all-reduce(f32[]{:T(128)} %get-tuple-element.32, f32[]{:T(128)} %get-tuple-element.33), channel_id=1, replica_groups=mesh['rows_0'=4,'rows_1'=8,'rows_2'=4,'rows_3'=2] {'rows_1'}, use_global_device_ids=true, to_apply=%region_2.0 | all-reduce | flops 2 | bytes 16 | tf_op jit(solution)/shard_map/psum | solution.py:32
  156.8 10.8 %all-reduce.7 = (f32[]{:T(128)}, f32[]{:T(128)}) all-reduce(f32[]{:T(128)} %get-tuple-element.16, f32[]{:T(128)} %get-tuple-element.17), channel_id=1, replica_groups=mesh['rows_0'=4,'rows_1'=8,'rows_2'=4,'rows_3'=2] {'rows_2'}, use_global_device_ids=true, to_apply=%region_3.0 | all-reduce | flops 2 | bytes 16 | tf_op jit(solution)/shard_map/psum | solution.py:32
  167.6 10.8 %all-reduce.15 = (f32[]{:T(128)}, f32[]{:T(128)}) all-reduce(f32[]{:T(128)} %get-tuple-element.24, f32[]{:T(128)} %get-tuple-element.25), channel_id=1, replica_groups=mesh['rows_0'=4,'rows_1'=8,'rows_2'=4,'rows_3'=2] {'rows_3'}, use_global_device_ids=true, to_apply=%region_4.0 | all-reduce | flops 2 | bytes 16 | tf_op jit(solution)/shard_map/psum | solution.py:32
  185.9 15.5 %fusion.24 = f32[128,1,128]{2,1,0:T(1,128)S(1)} fusion(f32[128,128,1]{1,2,0:T(1,128)S(1)} %bitcast.287, f32[128,128,128]{2,1,0:T(8,128)} %gather_fusion, f32[128]{0:T(128)S(1)} %copy-done.2), kind=kOutput, calls=%fused_computation.47 | convolution fusion | flops 27262976 | bytes 8520192 | tf_op jit(solution)/shard_map/nij,nj->ni/dot_general | solution.py:37
  206.3 15.5 %fusion.16 = f32[128,1,128]{2,1,0:T(1,128)S(1)} fusion(f32[128,128,1]{1,2,0:T(1,128)S(1)} %bitcast.339, f32[128,128,128]{2,1,0:T(8,128)} %gather_fusion.1, f32[128]{0:T(128)S(1)} %slice_bitcast_fusion.8), kind=kOutput, calls=%fused_computation.39 | convolution fusion | flops 27262976 | bytes 8520192 | tf_op jit(solution)/shard_map/nij,nj->ni/dot_general | solution.py:37
  226.0 35.7 %fusion.4 = f32[5,64,1,128]{3,2,1,0:T(1,128)S(1)} fusion(f32[5,64,128,1]{2,3,1,0:T(1,128)S(1)} %bitcast.330, f32[5,64,128,128]{3,2,1,0:T(8,128)} %bitcast.282, f32[5,64]{1,0:T(8,128)S(1)} %bitcast.314), kind=kOutput, calls=%fused_computation.27 | convolution fusion | flops 68157440 | bytes 21300480 | tf_op jit(solution)/shard_map/lhij,lhj->lhi/dot_general | solution.py:78
  270.9 13.4 %all-reduce.2 = (f32[]{:T(128)}, f32[]{:T(128)}) all-reduce(f32[]{:T(128)} %get-tuple-element.30, f32[]{:T(128)} %get-tuple-element.31), channel_id=1, replica_groups=mesh['rows_0'=4,'rows_1'=8,'rows_2'=4,'rows_3'=2] {'rows_1'}, use_global_device_ids=true, to_apply=%region_12.0 | all-reduce | flops 2 | bytes 16 | tf_op jit(solution)/shard_map/psum | solution.py:32
  292.6 12.0 %all-reduce.14 = (f32[]{:T(128)}, f32[]{:T(128)}) all-reduce(f32[]{:T(128)} %get-tuple-element.22, f32[]{:T(128)} %get-tuple-element.23), channel_id=1, replica_groups=mesh['rows_0'=4,'rows_1'=8,'rows_2'=4,'rows_3'=2] {'rows_3'}, use_global_device_ids=true, to_apply=%region_14.0 | all-reduce | flops 2 | bytes 16 | tf_op jit(solution)/shard_map/psum | solution.py:32
  314.2 15.5 %fusion.22 = f32[128,1,128]{2,1,0:T(1,128)S(1)} fusion(f32[128,128,1]{1,2,0:T(1,128)S(1)} %bitcast.294, f32[128,128,128]{2,1,0:T(8,128)} %gather_fusion, f32[128]{0:T(128)S(1)} %copy-done.2), kind=kOutput, calls=%fused_computation.45 | convolution fusion | flops 27262976 | bytes 8520192 | tf_op jit(solution)/shard_map/nij,nj->ni/dot_general | solution.py:37
  333.7 15.5 %fusion.14 = f32[128,1,128]{2,1,0:T(1,128)S(1)} fusion(f32[128,128,1]{1,2,0:T(1,128)S(1)} %bitcast.340, f32[128,128,128]{2,1,0:T(8,128)} %gather_fusion.1, f32[128]{0:T(128)S(1)} %slice_bitcast_fusion.8), kind=kOutput, calls=%fused_computation.37 | convolution fusion | flops 27262976 | bytes 8520192 | tf_op jit(solution)/shard_map/nij,nj->ni/dot_general | solution.py:37
  352.3 35.6 %fusion.2 = f32[5,64,1,128]{3,2,1,0:T(1,128)S(1)} fusion(f32[5,64,128,1]{2,3,1,0:T(1,128)S(1)} %bitcast.331, f32[5,64,128,128]{3,2,1,0:T(8,128)} %bitcast.283, f32[5,64]{1,0:T(8,128)S(1)} %bitcast.315), kind=kOutput, calls=%fused_computation.25 | convolution fusion | flops 68157440 | bytes 21300480 | tf_op jit(solution)/shard_map/lhij,lhj->lhi/dot_general | solution.py:78
  389.0 9.1 %all-reduce.9 = (f32[]{:T(128)}, f32[]{:T(128)}) all-reduce(f32[]{:T(128)} %get-tuple-element.5, f32[]{:T(128)} %get-tuple-element.4), channel_id=1, replica_groups=mesh['rows_0'=4,'rows_1'=8,'rows_2'=4,'rows_3'=2] {'rows_0'}, use_global_device_ids=true, to_apply=%region_21.0 | all-reduce | flops 2 | bytes 16 | tf_op jit(solution)/shard_map/psum | solution.py:32
  398.1 14.0 %all-reduce.1 = (f32[]{:T(128)}, f32[]{:T(128)}) all-reduce(f32[]{:T(128)} %get-tuple-element.28, f32[]{:T(128)} %get-tuple-element.29), channel_id=1, replica_groups=mesh['rows_0'=4,'rows_1'=8,'rows_2'=4,'rows_3'=2] {'rows_1'}, use_global_device_ids=true, to_apply=%region_22.0 | all-reduce | flops 2 | bytes 16 | tf_op jit(solution)/shard_map/psum | solution.py:32
  420.8 10.9 %all-reduce.13 = (f32[]{:T(128)}, f32[]{:T(128)}) all-reduce(f32[]{:T(128)} %get-tuple-element.20, f32[]{:T(128)} %get-tuple-element.21), channel_id=1, replica_groups=mesh['rows_0'=4,'rows_1'=8,'rows_2'=4,'rows_3'=2] {'rows_3'}, use_global_device_ids=true, to_apply=%region_24.0 | all-reduce | flops 2 | bytes 16 | tf_op jit(solution)/shard_map/psum | solution.py:32
  439.8 15.5 %fusion.20 = f32[128,1,128]{2,1,0:T(1,128)S(1)} fusion(f32[128,128,1]{1,2,0:T(1,128)S(1)} %bitcast.308, f32[128,128,128]{2,1,0:T(8,128)} %gather_fusion, f32[128]{0:T(128)S(1)} %copy-done.2), kind=kOutput, calls=%fused_computation.43 | convolution fusion | flops 27262976 | bytes 8520192 | tf_op jit(solution)/shard_map/nij,nj->ni/dot_general | solution.py:37
  460.5 15.5 %fusion.12 = f32[128,1,128]{2,1,0:T(1,128)S(1)} fusion(f32[128,128,1]{1,2,0:T(1,128)S(1)} %bitcast.337, f32[128,128,128]{2,1,0:T(8,128)} %gather_fusion.1, f32[128]{0:T(128)S(1)} %slice_bitcast_fusion.8), kind=kOutput, calls=%fused_computation.35 | convolution fusion | flops 27262976 | bytes 8520192 | tf_op jit(solution)/shard_map/nij,nj->ni/dot_general | solution.py:37
  480.0 35.7 %fusion = f32[5,64,1,128]{3,2,1,0:T(1,128)S(1)} fusion(f32[5,64,128,1]{2,3,1,0:T(1,128)S(1)} %bitcast.332, f32[5,64,128,128]{3,2,1,0:T(8,128)} %bitcast.284, f32[5,64]{1,0:T(8,128)S(1)} %bitcast.316), kind=kOutput, calls=%fused_computation.23 | convolution fusion | flops 68157440 | bytes 21300480 | tf_op jit(solution)/shard_map/lhij,lhj->lhi/dot_general | solution.py:78
  516.7 8.9 %all-reduce.8 = (f32[]{:T(128)}, f32[]{:T(128)}) all-reduce(f32[]{:T(128)} %get-tuple-element.3, f32[]{:T(128)} %get-tuple-element.2), channel_id=1, replica_groups=mesh['rows_0'=4,'rows_1'=8,'rows_2'=4,'rows_3'=2] {'rows_0'}, use_global_device_ids=true, to_apply=%region_31.0 | all-reduce | flops 2 | bytes 16 | tf_op jit(solution)/shard_map/psum | solution.py:32
  525.5 13.4 %all-reduce = (f32[]{:T(128)}, f32[]{:T(128)}) all-reduce(f32[]{:T(128)} %get-tuple-element.26, f32[]{:T(128)} %get-tuple-element.27), channel_id=1, replica_groups=mesh['rows_0'=4,'rows_1'=8,'rows_2'=4,'rows_3'=2] {'rows_1'}, use_global_device_ids=true, to_apply=%region_32.0 | all-reduce | flops 2 | bytes 16 | tf_op jit(solution)/shard_map/psum | solution.py:32
  546.8 12.4 %all-reduce.12 = (f32[]{:T(128)}, f32[]{:T(128)}) all-reduce(f32[]{:T(128)} %get-tuple-element.18, f32[]{:T(128)} %get-tuple-element.19), channel_id=1, replica_groups=mesh['rows_0'=4,'rows_1'=8,'rows_2'=4,'rows_3'=2] {'rows_3'}, use_global_device_ids=true, to_apply=%region_34.0 | all-reduce | flops 2 | bytes 16 | tf_op jit(solution)/shard_map/psum | solution.py:32
  (152 shorter events, 135.5 us)
Async XLA Ops:
  2.8 97.0 %collective-permute-start.2 = (f32[64,128]{1,0:T(8,128)S(1)}, f32[64,128]{1,0:T(8,128)S(1)}, u32[]{:S(2)}, u32[]{:S(2)}) collective-permute-start(f32[64,128]{1,0:T(8,128)S(1)} %gather_fusion.3), channel_id=1, source_target_pairs={{0,128},{1,129},{2,130},{3,131},{4,132},{5,133},{6,134},{7,135},{8... | collective-permute-start | bytes 98312 | tf_op jit(solution)/shard_map/ppermute | solution.py:27
  8.1 91.7 %collective-permute-start.3 = (f32[64,128]{1,0:T(8,128)S(1)}, f32[64,128]{1,0:T(8,128)S(1)}, u32[]{:S(2)}, u32[]{:S(2)}) collective-permute-start(f32[64,128]{1,0:T(8,128)S(1)} %gather_fusion.4), channel_id=1, source_target_pairs={{0,64},{1,65},{2,66},{3,67},{4,68},{5,69},{6,70},{7,71},{8,72},{9,... | collective-permute-start | bytes 98312 | tf_op jit(solution)/shard_map/ppermute | solution.py:27
  10.0 89.9 %collective-permute-start.4 = (f32[64,128]{1,0:T(8,128)S(1)}, f32[64,128]{1,0:T(8,128)S(1)}, u32[]{:S(2)}, u32[]{:S(2)}) collective-permute-start(f32[64,128]{1,0:T(8,128)S(1)} %gather_fusion.5), channel_id=1, source_target_pairs={{0,32},{1,33},{2,34},{3,35},{4,36},{5,37},{6,38},{7,39},{8,40},{9,... | collective-permute-start | bytes 98312 | tf_op jit(solution)/shard_map/ppermute | solution.py:27
  18.4 81.4 %collective-permute-start.5 = (f32[64,128]{1,0:T(8,128)S(1)}, f32[64,128]{1,0:T(8,128)S(1)}, u32[]{:S(2)}, u32[]{:S(2)}) collective-permute-start(f32[64,128]{1,0:T(8,128)S(1)} %gather_fusion.6), channel_id=1, source_target_pairs={{0,16},{1,17},{2,18},{3,19},{4,20},{5,21},{6,22},{7,23},{8,24},{9,... | collective-permute-start | bytes 98312 | tf_op jit(solution)/shard_map/ppermute | solution.py:27
  20.4 60.8 %collective-permute-start = (f32[1,128]{1,0:T(1,128)S(1)}, f32[1,128]{1,0:T(1,128)S(1)}, u32[]{:S(2)}, u32[]{:S(2)}) collective-permute-start(f32[1,128]{1,0:T(1,128)S(1)} %get-tuple-element.52), channel_id=1, source_target_pairs={{0,1},{1,2},{2,3},{3,4},{4,5},{5,6},{6,7},{7,8},{8,9},{9,10},{10,1... | collective-permute-start | bytes 1544 | tf_op jit(solution)/shard_map/ppermute | solution.py:18
  81.2 16.0 %collective-permute-start.1 = (f32[1,128]{1,0:T(1,128)S(1)}, f32[1,128]{1,0:T(1,128)S(1)}, u32[]{:S(2)}, u32[]{:S(2)}) collective-permute-start(f32[1,128]{1,0:T(1,128)S(1)} %get-tuple-element.53), channel_id=1, source_target_pairs={{1,0},{2,1},{3,2},{4,3},{5,4},{6,5},{7,6},{8,7},{9,8},{10,9},{11,1... | collective-permute-start | bytes 1544 | tf_op jit(solution)/shard_map/ppermute | solution.py:19
  181.0 44.9 %collective-permute-start.9 = (f32[64,128]{1,0:T(8,128)S(1)}, f32[64,128]{1,0:T(8,128)S(1)}, u32[]{:S(2)}, u32[]{:S(2)}) collective-permute-start(f32[64,128]{1,0:T(8,128)S(1)} %gather_fusion.8), channel_id=1, source_target_pairs={{0,128},{1,129},{2,130},{3,131},{4,132},{5,133},{6,134},{7,135},{8... | collective-permute-start | bytes 98312 | tf_op jit(solution)/shard_map/ppermute | solution.py:27
  181.9 44.1 %collective-permute-start.10 = (f32[64,128]{1,0:T(8,128)S(1)}, f32[64,128]{1,0:T(8,128)S(1)}, u32[]{:S(2)}, u32[]{:S(2)}) collective-permute-start(f32[64,128]{1,0:T(8,128)S(1)} %gather_fusion.9), channel_id=1, source_target_pairs={{0,64},{1,65},{2,66},{3,67},{4,68},{5,69},{6,70},{7,71},{8,72},{9,... | collective-permute-start | bytes 98312 | tf_op jit(solution)/shard_map/ppermute | solution.py:27
  183.2 23.1 %collective-permute-start.7 = (f32[1,128]{1,0:T(1,128)S(1)}, f32[1,128]{1,0:T(1,128)S(1)}, u32[]{:S(2)}, u32[]{:S(2)}) collective-permute-start(f32[1,128]{1,0:T(1,128)S(1)} %get-tuple-element.50), channel_id=1, source_target_pairs={{0,1},{1,2},{2,3},{3,4},{4,5},{5,6},{6,7},{7,8},{8,9},{9,10},{10,1... | collective-permute-start | bytes 1544 | tf_op jit(solution)/shard_map/ppermute | solution.py:18
  203.2 22.7 %collective-permute-start.11 = (f32[64,128]{1,0:T(8,128)S(1)}, f32[64,128]{1,0:T(8,128)S(1)}, u32[]{:S(2)}, u32[]{:S(2)}) collective-permute-start(f32[64,128]{1,0:T(8,128)S(1)} %gather_fusion.10), channel_id=1, source_target_pairs={{0,32},{1,33},{2,34},{3,35},{4,36},{5,37},{6,38},{7,39},{8,40},{9,... | collective-permute-start | bytes 98312 | tf_op jit(solution)/shard_map/ppermute | solution.py:27
  205.4 20.6 %collective-permute-start.12 = (f32[64,128]{1,0:T(8,128)S(1)}, f32[64,128]{1,0:T(8,128)S(1)}, u32[]{:S(2)}, u32[]{:S(2)}) collective-permute-start(f32[64,128]{1,0:T(8,128)S(1)} %gather_fusion.11), channel_id=1, source_target_pairs={{0,16},{1,17},{2,18},{3,19},{4,20},{5,21},{6,22},{7,23},{8,24},{9,... | collective-permute-start | bytes 98312 | tf_op jit(solution)/shard_map/ppermute | solution.py:27
  206.3 15.5 %collective-permute-start.8 = (f32[1,128]{1,0:T(1,128)S(1)}, f32[1,128]{1,0:T(1,128)S(1)}, u32[]{:S(2)}, u32[]{:S(2)}) collective-permute-start(f32[1,128]{1,0:T(1,128)S(1)} %get-tuple-element.51), channel_id=1, source_target_pairs={{1,0},{2,1},{3,2},{4,3},{5,4},{6,5},{7,6},{8,7},{9,8},{10,9},{11,1... | collective-permute-start | bytes 1544 | tf_op jit(solution)/shard_map/ppermute | solution.py:19
  310.1 41.8 %collective-permute-start.16 = (f32[64,128]{1,0:T(8,128)S(1)}, f32[64,128]{1,0:T(8,128)S(1)}, u32[]{:S(2)}, u32[]{:S(2)}) collective-permute-start(f32[64,128]{1,0:T(8,128)S(1)} %gather_fusion.13), channel_id=1, source_target_pairs={{0,128},{1,129},{2,130},{3,131},{4,132},{5,133},{6,134},{7,135},{8... | collective-permute-start | bytes 98312 | tf_op jit(solution)/shard_map/ppermute | solution.py:27
  310.8 41.1 %collective-permute-start.17 = (f32[64,128]{1,0:T(8,128)S(1)}, f32[64,128]{1,0:T(8,128)S(1)}, u32[]{:S(2)}, u32[]{:S(2)}) collective-permute-start(f32[64,128]{1,0:T(8,128)S(1)} %gather_fusion.14), channel_id=1, source_target_pairs={{0,64},{1,65},{2,66},{3,67},{4,68},{5,69},{6,70},{7,71},{8,72},{9,... | collective-permute-start | bytes 98312 | tf_op jit(solution)/shard_map/ppermute | solution.py:27
  311.3 22.4 %collective-permute-start.14 = (f32[1,128]{1,0:T(1,128)S(1)}, f32[1,128]{1,0:T(1,128)S(1)}, u32[]{:S(2)}, u32[]{:S(2)}) collective-permute-start(f32[1,128]{1,0:T(1,128)S(1)} %get-tuple-element.48), channel_id=1, source_target_pairs={{0,1},{1,2},{2,3},{3,4},{4,5},{5,6},{6,7},{7,8},{8,9},{9,10},{10,1... | collective-permute-start | bytes 1544 | tf_op jit(solution)/shard_map/ppermute | solution.py:18
  331.6 20.4 %collective-permute-start.18 = (f32[64,128]{1,0:T(8,128)S(1)}, f32[64,128]{1,0:T(8,128)S(1)}, u32[]{:S(2)}, u32[]{:S(2)}) collective-permute-start(f32[64,128]{1,0:T(8,128)S(1)} %gather_fusion.15), channel_id=1, source_target_pairs={{0,32},{1,33},{2,34},{3,35},{4,36},{5,37},{6,38},{7,39},{8,40},{9,... | collective-permute-start | bytes 98312 | tf_op jit(solution)/shard_map/ppermute | solution.py:27
  333.0 19.0 %collective-permute-start.19 = (f32[64,128]{1,0:T(8,128)S(1)}, f32[64,128]{1,0:T(8,128)S(1)}, u32[]{:S(2)}, u32[]{:S(2)}) collective-permute-start(f32[64,128]{1,0:T(8,128)S(1)} %gather_fusion.16), channel_id=1, source_target_pairs={{0,16},{1,17},{2,18},{3,19},{4,20},{5,21},{6,22},{7,23},{8,24},{9,... | collective-permute-start | bytes 98312 | tf_op jit(solution)/shard_map/ppermute | solution.py:27
  333.7 15.5 %collective-permute-start.15 = (f32[1,128]{1,0:T(1,128)S(1)}, f32[1,128]{1,0:T(1,128)S(1)}, u32[]{:S(2)}, u32[]{:S(2)}) collective-permute-start(f32[1,128]{1,0:T(1,128)S(1)} %get-tuple-element.49), channel_id=1, source_target_pairs={{1,0},{2,1},{3,2},{4,3},{5,4},{6,5},{7,6},{8,7},{9,8},{10,9},{11,1... | collective-permute-start | bytes 1544 | tf_op jit(solution)/shard_map/ppermute | solution.py:19
  436.7 43.1 %collective-permute-start.23 = (f32[64,128]{1,0:T(8,128)S(1)}, f32[64,128]{1,0:T(8,128)S(1)}, u32[]{:S(2)}, u32[]{:S(2)}) collective-permute-start(f32[64,128]{1,0:T(8,128)S(1)} %gather_fusion.18), channel_id=1, source_target_pairs={{0,128},{1,129},{2,130},{3,131},{4,132},{5,133},{6,134},{7,135},{8... | collective-permute-start | bytes 98312 | tf_op jit(solution)/shard_map/ppermute | solution.py:27
  437.4 42.5 %collective-permute-start.24 = (f32[64,128]{1,0:T(8,128)S(1)}, f32[64,128]{1,0:T(8,128)S(1)}, u32[]{:S(2)}, u32[]{:S(2)}) collective-permute-start(f32[64,128]{1,0:T(8,128)S(1)} %gather_fusion.19), channel_id=1, source_target_pairs={{0,64},{1,65},{2,66},{3,67},{4,68},{5,69},{6,70},{7,71},{8,72},{9,... | collective-permute-start | bytes 98312 | tf_op jit(solution)/shard_map/ppermute | solution.py:27
  437.4 23.1 %collective-permute-start.21 = (f32[1,128]{1,0:T(1,128)S(1)}, f32[1,128]{1,0:T(1,128)S(1)}, u32[]{:S(2)}, u32[]{:S(2)}) collective-permute-start(f32[1,128]{1,0:T(1,128)S(1)} %get-tuple-element.46), channel_id=1, source_target_pairs={{0,1},{1,2},{2,3},{3,4},{4,5},{5,6},{6,7},{7,8},{8,9},{9,10},{10,1... | collective-permute-start | bytes 1544 | tf_op jit(solution)/shard_map/ppermute | solution.py:18
  457.2 22.7 %collective-permute-start.25 = (f32[64,128]{1,0:T(8,128)S(1)}, f32[64,128]{1,0:T(8,128)S(1)}, u32[]{:S(2)}, u32[]{:S(2)}) collective-permute-start(f32[64,128]{1,0:T(8,128)S(1)} %gather_fusion.20), channel_id=1, source_target_pairs={{0,32},{1,33},{2,34},{3,35},{4,36},{5,37},{6,38},{7,39},{8,40},{9,... | collective-permute-start | bytes 98312 | tf_op jit(solution)/shard_map/ppermute | solution.py:27
  460.5 19.5 %collective-permute-start.26 = (f32[64,128]{1,0:T(8,128)S(1)}, f32[64,128]{1,0:T(8,128)S(1)}, u32[]{:S(2)}, u32[]{:S(2)}) collective-permute-start(f32[64,128]{1,0:T(8,128)S(1)} %gather_fusion.21), channel_id=1, source_target_pairs={{0,16},{1,17},{2,18},{3,19},{4,20},{5,21},{6,22},{7,23},{8,24},{9,... | collective-permute-start | bytes 98312 | tf_op jit(solution)/shard_map/ppermute | solution.py:27
  460.5 15.6 %collective-permute-start.22 = (f32[1,128]{1,0:T(1,128)S(1)}, f32[1,128]{1,0:T(1,128)S(1)}, u32[]{:S(2)}, u32[]{:S(2)}) collective-permute-start(f32[1,128]{1,0:T(1,128)S(1)} %get-tuple-element.47), channel_id=1, source_target_pairs={{1,0},{2,1},{3,2},{4,3},{5,4},{6,5},{7,6},{8,7},{9,8},{10,9},{11,1... | collective-permute-start | bytes 1544 | tf_op jit(solution)/shard_map/ppermute | solution.py:19
  (8 other events, 82.4 us)
where the time goes:
time: 568 us; the launch traced here: 564 us
  matrix products  278 us (49%)
  blocking collectives  169 us (30%)
  local copies, waits for them, and re-layouts  53.9 us (9%)
  starting transfers between devices  43 us (8%)
  between operations  16.5 us (3%)
    psum x16, blocking collectives, one_axis_at_a_time(): array = lax.psum(array, axis)  169 us
    dot_general x4, matrix products, operate(): jnp.einsum('lhij,lhj->lhi', link_mats, jnp.stack(differences), precision=...  143 us
    dot_general x8, matrix products, batched(): jnp.einsum('nij,nj->ni', mats, vectors, precision=lax.Precision.HIGHEST)  124 us
    ppermute x20, starting transfers between devices, from_partner(): return lax.ppermute(value, axis, pairs)  31.4 us
    gather x1, local copies, waits for them, and re-layouts, per_device(): link_mats = dictionary[link_ids[0]] * link_weights[0][:, :, None, None]  17.2 us
    gather x20, local copies, waits for them, and re-layouts, operate(): own_part = block_vec[own_rows[level_idx]]  16.2 us
  transfers between devices with their start and end apart: 28, of which 2 were waited for; matrix products, arithmetic and copies ran while one was open for 32% of the time, Pallas kernels for 0%

commit v1 on v0

v1 whole, which is shorter than its diff:
```python
import functools

import jax
import jax.numpy as jnp
from jax import lax
from jax.experimental import pallas as pl
from jax.experimental.pallas import tpu as pltpu
from jax.sharding import PartitionSpec as P

AXIS = "rows"
MESH = pl.DeviceIdType.MESH
ITERS = 4
BS = 128
NB = 128
HALF = 64
LEVELS = 5
LINKS = LEVELS * HALF
LEVEL_OF = (4, 1, 3, 0, 2)
EDGE0 = NB
LINK0 = 2 * NB
BOUND0 = LINK0 + 3 * NB
TOTAL = BOUND0 + NB
PARTS = 16
F32 = jnp.float32
BF16 = jnp.bfloat16


def level_mask(li):
    q = li // 2
    return 8 * (1 + q + q // 2) * (1 + 7 * (li % 2))


def level_partner(me, li):
    mask = level_mask(li)
    return me + mask - 2 * mask * ((me // mask) % 2)


def split_rows(d):
    high = d.astype(BF16).astype(F32)
    return jnp.concatenate([high, d - high], axis=0).astype(BF16)


def kernel(
    ids, rows, b_ref, shift_ref, dict_ref, wrow_ref, lrow_ref,
    x_ref, r_ref,
    g_ref, stage, wv, st, upad, w_ref, p_ref, s_ref, z_ref, acc_ref, f_ref, ol_ref, scal,
    send, recv, csend, crecv, ar_src, ar_one, ar_mid, ar_two,
    dict_sem, lv_s, lv_r, cy_s, cy_r, a1_s, a1_r, a2_s, a2_r,
):
    me = lax.axis_index(AXIS)
    n = lax.axis_size(AXIS)
    core, xs, zs, ys = me % 2, (me // 2) % 4, (me // 8) % 8, me // 64
    nxt, prv = (me + 1) % n, (me + n - 1) % n

    def one_peer(j):
        return ys * 64 + ((zs + j // 2) % 8) * 8 + xs * 2 + (core + j % 2) % 2

    def two_peer(j):
        return ((ys + j // 4) % 4) * 64 + zs * 8 + ((xs + j % 4) % 4) * 2 + core

    def dict_copy(c):
        part = pl.ds(c * 8, 8)
        return pltpu.make_async_copy(dict_ref.at[part], stage.at[part], dict_sem.at[c])

    @pl.loop(0, 16)
    def _(c):
        dict_copy(c).start()

    barrier = pltpu.get_barrier_semaphore()

    @pl.loop(1, PARTS)
    def _(j):
        pl.semaphore_signal(barrier, inc=1, device_id={AXIS: one_peer(j)}, device_id_type=MESH)
        pl.semaphore_signal(barrier, inc=1, device_id={AXIS: two_peer(j)}, device_id_type=MESH)

    pl.semaphore_signal(barrier, inc=1, device_id={AXIS: nxt}, device_id_type=MESH)
    pl.semaphore_signal(barrier, inc=1, device_id={AXIS: prv}, device_id_type=MESH)

    eye = lax.broadcasted_iota(jnp.int32, (NB, BS), 0) == lax.broadcasted_iota(jnp.int32, (NB, BS), 1)
    for blk in range(6):
        column = jnp.sum(jnp.where(eye, wrow_ref[blk : blk + 1, :], 0.0), axis=1, keepdims=True)
        wv[blk * NB : (blk + 1) * NB, :] = jnp.broadcast_to(column, (NB, BS))
    for blk in range(3):
        cols = slice(blk * BS, (blk + 1) * BS)
        hit = lax.broadcasted_iota(jnp.int32, (NB, BS), 0) == lrow_ref[0:1, cols]
        st[:, cols] = jnp.where(hit, 1.0, 0.0).astype(BF16)
    zeros = jnp.zeros((NB, BS), F32)
    upad[0:8, :] = jnp.zeros((8, BS), F32)
    upad[8 : 8 + NB, :] = b_ref[...]
    x_ref[...] = zeros
    r_ref[...] = b_ref[...]
    p_ref[...] = zeros
    s_ref[...] = zeros
    z_ref[...] = zeros
    ol_ref[LINKS:, :] = jnp.zeros((64, 2 * BS), F32)
    scal[...] = jnp.ones((2, 8, BS), F32)

    @pl.loop(0, 16)
    def _(c):
        dict_copy(c).wait()

        @pl.loop(0, 8)
        def _(i):
            block = stage[c * 8 + i]
            high = block.astype(BF16)
            g_ref[c * 8 + i, :, 0:BS] = high
            g_ref[c * 8 + i, :, BS:] = (block - high.astype(F32)).astype(BF16)

    pl.semaphore_wait(barrier, 2 * (PARTS - 1) + 2)

    sub16 = lax.broadcasted_iota(jnp.int32, (16, BS), 0) % 8

    def products(d, base, count):
        lhs = split_rows(d)
        out = jnp.zeros((16, 2 * BS), F32)
        for j in range(count):
            picked = jnp.where(sub16 == j, lhs, jnp.zeros_like(lhs))
            out = out + jnp.dot(picked, g_ref[ids[base + j]], preferred_element_type=F32)
        return out[:8, :BS] + out[:8, BS:] + out[8:, :BS]

    def level_copy(k, li):
        return pltpu.make_async_remote_copy(
            src_ref=send.at[k, li], dst_ref=recv.at[k, li], send_sem=lv_s.at[k, li], recv_sem=lv_r.at[k, li],
            device_id={AXIS: level_partner(me, li)}, device_id_type=MESH)

    def cycle_copy(k, side):
        return pltpu.make_async_remote_copy(
            src_ref=csend.at[k, side], dst_ref=crecv.at[k, side], send_sem=cy_s.at[k, side],
            recv_sem=cy_r.at[k, side], device_id={AXIS: nxt if side == 0 else prv}, device_id_type=MESH)

    def one_copy(k, j):
        return pltpu.make_async_remote_copy(
            src_ref=ar_src.at[k], dst_ref=ar_one.at[k, j], send_sem=a1_s.at[k, j], recv_sem=a1_r.at[k, j],
            device_id={AXIS: one_peer(j)}, device_id_type=MESH)

    def two_copy(k, j):
        return pltpu.make_async_remote_copy(
            src_ref=ar_mid.at[k], dst_ref=ar_two.at[k, j], send_sem=a2_s.at[k, j], recv_sem=a2_r.at[k, j],
            device_id={AXIS: two_peer(j)}, device_id_type=MESH)

    def reduce_begin(k):
        @pl.loop(1, PARTS)
        def _(j):
            one_copy(k, j).start()

    def reduce_middle(k):
        @pl.loop(1, PARTS)
        def _(j):
            one_copy(k, j).wait()

        ar_one[k, 0] = ar_src[k]
        ar_mid[k] = jnp.sum(ar_one[k], axis=0)

        @pl.loop(1, PARTS)
        def _(j):
            two_copy(k, j).start()

    def reduce_end(k):
        @pl.loop(1, PARTS)
        def _(j):
            two_copy(k, j).wait()

        ar_two[k, 0] = ar_mid[k]
        total = jnp.sum(ar_two[k], axis=0)
        sums = jnp.sum(total, axis=1, keepdims=True)
        norm = jnp.broadcast_to(sums[0:1, :], (8, BS))
        product = jnp.broadcast_to(sums[1:2, :], (8, BS))
        return norm, product

    def coefficients(k, norm, product):
        first = jnp.where(k == 0, 0.0, 1.0).astype(F32)
        beta = first * (norm / scal[0])
        alpha = norm / (product - beta * norm / scal[1])
        scal[0] = norm
        scal[1] = alpha
        return alpha, beta

    def put_sums(k):
        r = r_ref[...]
        ar_src[k, 0:1, :] = jnp.sum(r * r, axis=0, keepdims=True)
        ar_src[k, 1:2, :] = jnp.sum(r * w_ref[...], axis=0, keepdims=True)

    def operate(k):
        @pl.loop(0, LEVELS)
        def _(i):
            li = LEVELS - 1 - i

            @pl.loop(0, HALF // 16)
            def _(h):
                for j in range(16):
                    row = rows[li * HALF + h * 16 + j]
                    send[k, li, pl.ds(h * 16 + j, 1), :] = upad[pl.ds(row + 8, 1), :]

            level_copy(k, li).start()

        csend[k, 0] = upad[7 + NB : 8 + NB, :]
        csend[k, 1] = upad[8:9, :]
        cycle_copy(k, 0).start()
        cycle_copy(k, 1).start()

        def local(t, carry):
            for half in range(4):
                g = pl.multiple_of(t * 32 + half * 8, 8)
                here = upad[pl.ds(g + 8, 8), :]
                before = upad[pl.ds(g + 7, 8), :]
                acc_ref[pl.ds(g, 8), :] = shift_ref[pl.ds(g, 8), :] * here + products(
                    here * wv[pl.ds(g, 8), :], g, 8
                )
                f_ref[pl.ds(g, 8), :] = products((here - before) * wv[pl.ds(EDGE0 + g, 8), :], EDGE0 + g, 8)
            return carry

        lax.fori_loop(0, 4, local, 0)

        @pl.when(k > 0)
        def _():
            reduce_middle(k - 1)

        def level(li, carry):
            level_copy(k, li).wait_recv()
            for h in range(8):
                c = pl.multiple_of(li * HALF + h * 8, 8)
                diff = send[k, li, h * 8 : h * 8 + 8, :] - recv[k, li, h * 8 : h * 8 + 8, :]
                out = products(diff * wv[pl.ds(LINK0 + c, 8), :], LINK0 + c, 8)
                high = out.astype(BF16).astype(F32)
                ol_ref[pl.ds(c, 8), 0:BS] = high
                ol_ref[pl.ds(c, 8), BS:] = out - high
            return carry

        lax.fori_loop(0, LEVELS, level, 0)
        cycle_copy(k, 0).wait()
        cycle_copy(k, 1).wait()
        sub8 = lax.broadcasted_iota(jnp.int32, (8, BS), 0)
        edge = jnp.where(sub8 == 0, upad[8:9, :] - crecv[k, 0], crecv[k, 1] - upad[7 + NB : 8 + NB, :])
        bound = products(edge * wv[BOUND0 : BOUND0 + 8, :], BOUND0, 2)
        f_ref[0:1, :] = bound[0:1, :]
        f_ref[NB : NB + 1, :] = bound[1:2, :]
        spread = jnp.dot(st[...], ol_ref[...].astype(BF16), preferred_element_type=F32)
        acc_ref[...] = acc_ref[...] + (f_ref[0:NB, :] - f_ref[1 : NB + 1, :]) + (spread[:, :BS] + spread[:, BS:])

        @pl.loop(0, LEVELS)
        def _(li):
            level_copy(k, li).wait_send()


    def iteration(k, carry):
        @pl.when(k > 0)
        def _():
            reduce_begin(k - 1)

        operate(k)

        @pl.when(k == 0)
        def _():
            w_ref[...] = acc_ref[...]

        @pl.when(k > 0)
        def _():
            alpha, beta = coefficients(k - 1, *reduce_end(k - 1))
            alpha, beta = jnp.tile(alpha, (16, 1)), jnp.tile(beta, (16, 1))
            p = r_ref[...] + beta * p_ref[...]
            s = w_ref[...] + beta * s_ref[...]
            z = acc_ref[...] + beta * z_ref[...]
            p_ref[...] = p
            s_ref[...] = s
            z_ref[...] = z
            x_ref[...] = x_ref[...] + alpha * p
            r_ref[...] = r_ref[...] - alpha * s
            w_ref[...] = w_ref[...] - alpha * z

        upad[8 : 8 + NB, :] = w_ref[...]
        put_sums(k)
        return carry

    lax.fori_loop(0, ITERS, iteration, 0)
    last = ITERS - 1
    reduce_begin(last)
    reduce_middle(last)
    alpha, beta = coefficients(last, *reduce_end(last))
    alpha, beta = jnp.tile(alpha, (16, 1)), jnp.tile(beta, (16, 1))
    x_ref[...] = x_ref[...] + alpha * (r_ref[...] + beta * p_ref[...])
    r_ref[...] = r_ref[...] - alpha * (w_ref[...] + beta * s_ref[...])


def per_device(
    right_side,
    diag_shift,
    dictionary,
    diag_ids,
    diag_gain,
    cycle_ids,
    cycle_weights,
    link_rows,
    link_ids,
    link_weights,
):

    def reordered(values):
        return jnp.concatenate([values[0, m] for m in LEVEL_OF])

    def table(diag, cycle, link):
        return jnp.concatenate(
            [diag, cycle[:, 0], reordered(link), jnp.zeros((64,), diag.dtype), cycle[0, :1], cycle[-1, 1:],
             jnp.zeros((126,), diag.dtype)])

    ids = table(diag_ids, cycle_ids, link_ids)
    weights = table(diag_gain, cycle_weights, link_weights).reshape(6, BS)
    rows = jnp.concatenate([reordered(link_rows), jnp.full((64,), -1, jnp.int32)])
    vec = (NB, BS)
    smem = pl.BlockSpec(memory_space=pltpu.SMEM)
    vmem = pl.BlockSpec(memory_space=pltpu.VMEM)
    solved, residual = pl.pallas_call(
        kernel,
        out_shape=(jax.ShapeDtypeStruct(vec, F32), jax.ShapeDtypeStruct(vec, F32)),
        in_specs=[smem, smem, vmem, vmem, pl.BlockSpec(memory_space=pl.ANY), vmem, vmem],
        out_specs=(vmem, vmem),
        scratch_shapes=[
            pltpu.VMEM((BS, BS, 2 * BS), BF16),
            pltpu.VMEM((BS, BS, BS), F32),
            pltpu.VMEM((TOTAL, BS), F32),
            pltpu.VMEM((NB, 3 * BS), BF16),
            pltpu.VMEM((NB + 8, BS), F32),
            pltpu.VMEM(vec, F32),
            pltpu.VMEM(vec, F32),
            pltpu.VMEM(vec, F32),
            pltpu.VMEM(vec, F32),
            pltpu.VMEM(vec, F32),
            pltpu.VMEM((NB + 8, BS), F32),
            pltpu.VMEM((3 * BS, 2 * BS), F32),
            pltpu.VMEM((2, 8, BS), F32),
            pltpu.VMEM((ITERS, LEVELS, HALF, BS), F32),
            pltpu.VMEM((ITERS, LEVELS, HALF, BS), F32),
            pltpu.VMEM((ITERS, 2, 1, BS), F32),
            pltpu.VMEM((ITERS, 2, 1, BS), F32),
            pltpu.VMEM((ITERS, 2, BS), F32),
            pltpu.VMEM((ITERS, PARTS, 2, BS), F32),
            pltpu.VMEM((ITERS, 2, BS), F32),
            pltpu.VMEM((ITERS, PARTS, 2, BS), F32),
            pltpu.SemaphoreType.DMA((16,)),
            pltpu.SemaphoreType.DMA((ITERS, LEVELS)),
            pltpu.SemaphoreType.DMA((ITERS, LEVELS)),
            pltpu.SemaphoreType.DMA((ITERS, 2)),
            pltpu.SemaphoreType.DMA((ITERS, 2)),
            pltpu.SemaphoreType.DMA((ITERS, PARTS)),
            pltpu.SemaphoreType.DMA((ITERS, PARTS)),
            pltpu.SemaphoreType.DMA((ITERS, PARTS)),
            pltpu.SemaphoreType.DMA((ITERS, PARTS)),
        ],
        compiler_params=pltpu.CompilerParams(
            collective_id=0, has_side_effects=True, vmem_limit_bytes=40 * 1024 * 1024
        ),
        name="cg",
    )(ids, rows, right_side.reshape(vec), diag_shift.reshape(vec), dictionary, weights, rows.reshape(1, 3 * BS))
    return solved.reshape(-1), residual.reshape(-1)


def solution(mesh):
    placed = (
        P(AXIS),
        P(AXIS),
        P(),
        P(AXIS),
        P(AXIS),
        P(AXIS, None),
        P(AXIS, None),
        P(AXIS, None, None),
        P(AXIS, None, None),
        P(AXIS, None, None),
    )
    return jax.shard_map(
        per_device, mesh=mesh, in_specs=placed, out_specs=(P(AXIS), P(AXIS)), check_vma=False
    )
```

time: 568 us -> 79.6 us (0.14)
  matrix products: 278 us -> 0 us
  blocking collectives: 169 us -> 0 us
  Pallas kernels: 0 us -> 61.8 us
  starting transfers between devices: 43 us -> 0 us
  local copies, waits for them, and re-layouts: 53.9 us -> 16.8 us
  between operations: 16.5 us -> 0.65 us
    dot_general x20 -> x0, matrix products: 278 us -> none  [the longest x4 143 us: operate(): jnp.einsum('lhij,lhj->lhi', link_mats, jnp.stack(differences), precision=...]
    psum x16 -> x0, blocking collectives: 169 us -> none  [one_axis_at_a_time(): array = lax.psum(array, axis)]
    pallas_call x0 -> x1, Pallas kernels: none -> 61.8 us  [per_device(): pl.pallas_call(kernel, out_shape=(jax.ShapeDtypeStruct(vec, F32), jax.Sha...]
    gather x23 -> x0, local copies, waits for them, and re-layouts: 49 us -> none  [the longest x1 17.2 us: per_device(): link_mats = dictionary[link_ids[0]] * link_weights[0][:, :, None, None]]
    ppermute x28 -> x0, starting transfers between devices: 43 us -> none  [the longest x20 31.4 us: from_partner(): return lax.ppermute(value, axis, pairs)]
  transfers between devices with their start and end apart: 28 -> 0, of which waited for: 2 -> 0; matrix products, arithmetic and copies ran while one was open for 32% -> 0% of each run, Pallas kernels for 0% -> 0%
where the time goes in v1:
time: 79.6 us; the launch traced here: 79.2 us
  Pallas kernels  61.8 us (78%)
  local copies, waits for them, and re-layouts  16.8 us (21%)
    pallas_call x1, Pallas kernels, per_device(): pl.pallas_call(kernel, out_shape=(jax.ShapeDtypeStruct(vec, F32), jax.Sha...  61.8 us
    unnamed x8, local copies, waits for them, and re-layouts  6.33 us
    concatenate x2, local copies, waits for them, and re-layouts, table(): jnp.concatenate([diag, cycle[:, 0], reordered(link), jnp.zeros((64,), dia...  4.06 us
    slice x2, local copies, waits for them, and re-layouts, table(): cycle[-1, 1:]  2.74 us
    squeeze x3, local copies, waits for them, and re-layouts, reordered(): return jnp.concatenate([values[0, m] for m in LEVEL_OF])  2.17 us

profile of v1, /device:TPU:1, one launch (start us, length us, event | category | flops | bytes accessed | tf_op | source)
XLA Modules:
  0.0 79.2 jit_solution(4027935548591076199)
XLA Ops:
  0.6 0.7 slice_bitcast_fusion.16
  1.3 0.7 slice_bitcast_fusion.5
  2.0 1.3 %fusion.1 = (s32[1,1]{0,1:T(1,128)}, s32[1,1]{0,1:T(1,128)}) fusion(s32[128,2]{0,1:T(2,128)} %param.15), kind=kLoop, calls=%fused_computation.18 | loop fusion | bytes 16 | tf_op jit(solution)/shard_map/slice | solution.py:302
  3.3 1.4 %fusion = (f32[1,1]{0,1:T(1,128)}, f32[1,1]{0,1:T(1,128)}) fusion(f32[128,2]{0,1:T(2,128)} %param.16), kind=kLoop, calls=%fused_computation.17 | loop fusion | bytes 16 | tf_op jit(solution)/shard_map/slice | solution.py:302
  4.7 0.7 slice_bitcast_fusion.6
  5.5 0.1 concatenate.10.rows
  5.5 0.7 slice_bitcast_fusion.11
  6.3 2.0 %concatenate.9.ids = s32[768]{0:T(1024)S(1)} concatenate(s32[128]{0:T(128)} %param.13, s32[128]{0:T(128)S(1)} %slice_bitcast_fusion.16, s32[64]{0:T(128)S(1)} %get-tuple-element.19, s32[64]{0:T(128)S(1)} %get-tuple-element.18, s32[64]{0:T(128)S(1)} %get-tuple-element.17, s32[64]{0:T(128)S(1)} %get-tuple-element.20, s32[64]{0:T(128)S(1)} %get-tuple-element.16, ...), dimensions={0} | concatenate | bytes 6144 | tf_op jit(solution)/shard_map/concatenate | solution.py:301
  8.3 0.7 slice_bitcast_fusion
  9.0 2.0 %concatenate.11 = f32[768]{0:T(1024)S(1)} concatenate(f32[128]{0:T(128)} %param.14, f32[128]{0:T(128)S(1)} %slice_bitcast_fusion.5, f32[64]{0:T(128)S(1)} %get-tuple-element.9, f32[64]{0:T(128)S(1)} %get-tuple-element.8, f32[64]{0:T(128)S(1)} %get-tuple-element.7, f32[64]{0:T(128)S(1)} %get-tuple-element.10, f32[64]{0:T(128)S(1)} %get-tuple-element.6, f32[64]{0:T(128)S(1)} %broadcast_in_dim.18, ...), dimensions={0} | concatenate | bytes 6144 | tf_op jit(solution)/shard_map/concatenate | solution.py:301
  11.1 0.0 copy-start
  11.1 3.4 %copy-done = f32[128,128,128]{2,1,0:T(8,128)S(1)} copy-done((f32[128,128,128]{2,1,0:T(8,128)S(1)}, f32[128,128,128]{2,1,0:T(8,128)}, u32[]{:S(2)}) %copy-start) | copy-done | bytes 8388632
  14.5 0.0 copy-start.1
  14.5 0.8 %copy-done.1 = f32[16384]{0:T(1024)S(1)} copy-done((f32[16384]{0:T(1024)S(1)}, f32[16384]{0:T(1024)}, u32[]{:S(2)}) %copy-start.1) | copy-done | bytes 65560
  15.3 0.0 copy-start.2
  15.3 0.8 %copy-done.2 = f32[16384]{0:T(1024)S(1)} copy-done((f32[16384]{0:T(1024)S(1)}, f32[16384]{0:T(1024)}, u32[]{:S(2)}) %copy-start.2) | copy-done | bytes 65560
  16.1 61.8 %cg.1 = (f32[128,128]{1,0:T(8,128)S(1)}, f32[128,128]{1,0:T(8,128)S(1)}) custom-call(s32[768]{0:T(1024)S(1)} %concatenate.9.ids, s32[384]{0:T(512)S(1)} %concatenate.10.rows, f32[128,128]{1,0:T(8,128)S(1)} %bitcast.43, f32[128,128]{1,0:T(8,128)S(1)} %bitcast.44, f32[128,128,128]{2,1,0:T(8,128)S(1)} %copy-done, f32[6,128]{1,0:T(8,128)S(1)} %bitcast.47, ...), custom_call_target="tpu_custom_call" | custom-call | tf_op jit(solution)/shard_map/cg/pallas_call | solution.py:311
  77.9 0.6 copy.14
  78.6 0.6 copy.15
  (6 shorter events, 0.0 us)
Async XLA Ops:
  11.1 3.4 %copy-start = (f32[128,128,128]{2,1,0:T(8,128)S(1)}, f32[128,128,128]{2,1,0:T(8,128)}, u32[]{:S(2)}) copy-start(f32[128,128,128]{2,1,0:T(8,128)} %dict_ref.1) | copy-start | bytes 25165828
  14.5 0.8 %copy-start.1 = (f32[16384]{0:T(1024)S(1)}, f32[16384]{0:T(1024)}, u32[]{:S(2)}) copy-start(f32[16384]{0:T(1024)} %param.10) | copy-start | bytes 196612
  15.3 0.8 %copy-start.2 = (f32[16384]{0:T(1024)S(1)}, f32[16384]{0:T(1024)}, u32[]{:S(2)}) copy-start(f32[16384]{0:T(1024)} %param.11) | copy-start | bytes 196612

commit v2 on v1

v2 whole, which is shorter than its diff:
```python
import functools

import jax
import jax.numpy as jnp
from jax import lax
from jax.experimental import pallas as pl
from jax.experimental.pallas import tpu as pltpu
from jax.sharding import PartitionSpec as P

AXIS = "rows"
MESH = pl.DeviceIdType.MESH
ITERS = 4
BS = 128
NB = 128
HALF = 64
LEVELS = 5
LINKS = LEVELS * HALF
EDGE0 = NB
LINK0 = 2 * NB
SUMS = 3
PARTS = 16
F32 = jnp.float32
BF16 = jnp.bfloat16


def level_mask(li):
    q = li // 2
    return 8 * (1 + q + q // 2) * (1 + 7 * (li % 2))


def level_index(li):
    return 4 - li // 2 - 3 * (li % 2)


def level_partner(me, li):
    mask = level_mask(li)
    return me + mask - 2 * mask * ((me // mask) % 2)


def split_rows(d):
    high = d.astype(BF16).astype(F32)
    return jnp.concatenate([high, d - high], axis=0).astype(BF16)


def kernel(
    b_hbm, shift_hbm, dict_hbm, dids_hbm, gain_hbm, cids_hbm, cw_hbm, lrow_hbm, lids_hbm, lw_hbm,
    x_ref, r_ref,
    g_ref, stage, shift_ref, dids, cids, rows, lids, gain, cw, lrow, lw,
    wv, bw, st, upad, vecs, acc_ref, f_ref, ol_ref, scal,
    send, recv, csend, crecv, ar_src, ar_one, ar_mid, ar_two,
    in_sem, dict_sem, lv_s, lv_r, cy_s, cy_r, a1_s, a1_r, a2_s, a2_r,
):
    me = lax.axis_index(AXIS)
    n = lax.axis_size(AXIS)
    core, xs, zs, ys = me % 2, (me // 2) % 4, (me // 8) % 8, me // 64
    nxt, prv = (me + 1) % n, (me + n - 1) % n

    def one_peer(j):
        return ys * 64 + ((zs + j // 2) % 8) * 8 + xs * 2 + (core + j % 2) % 2

    def two_peer(j):
        return ((ys + j // 4) % 4) * 64 + zs * 8 + ((xs + j % 4) % 4) * 2 + core

    small = [
        pltpu.make_async_copy(src, dst, in_sem.at[i])
        for i, (src, dst) in enumerate((
            (b_hbm, upad.at[pl.ds(8, NB)]), (lrow_hbm, rows), (lrow_hbm, lrow), (shift_hbm, shift_ref),
            (gain_hbm, gain), (cw_hbm, cw), (lw_hbm, lw), (dids_hbm, dids), (cids_hbm, cids), (lids_hbm, lids),
        ))
    ]
    for copy in small:
        copy.start()

    def dict_copy(c):
        part = pl.ds(c * 8, 8)
        return pltpu.make_async_copy(dict_hbm.at[part], stage.at[part], dict_sem.at[c])

    @pl.loop(0, 16)
    def _(c):
        dict_copy(c).start()

    barrier = pltpu.get_barrier_semaphore()

    @pl.loop(1, PARTS)
    def _(j):
        pl.semaphore_signal(barrier, inc=1, device_id={AXIS: one_peer(j)}, device_id_type=MESH)
        pl.semaphore_signal(barrier, inc=1, device_id={AXIS: two_peer(j)}, device_id_type=MESH)

    pl.semaphore_signal(barrier, inc=1, device_id={AXIS: nxt}, device_id_type=MESH)
    pl.semaphore_signal(barrier, inc=1, device_id={AXIS: prv}, device_id_type=MESH)

    for copy in small:
        copy.wait()

    eye = lax.broadcasted_iota(jnp.int32, (NB, BS), 0) == lax.broadcasted_iota(jnp.int32, (NB, BS), 1)
    row_of = lax.broadcasted_iota(jnp.int32, (NB, BS), 0)

    def spread_rows(row):
        return jnp.broadcast_to(jnp.sum(jnp.where(eye, row, 0.0), axis=1, keepdims=True), (NB, BS))

    wv[0:NB, :] = spread_rows(gain[...])
    wv[EDGE0 : EDGE0 + NB, :] = spread_rows(cw[0:1, :])
    for blk in range(3):
        m0, m1 = level_index(2 * blk), level_index(min(2 * blk + 1, LEVELS - 1))
        lanes = slice(blk * BS, (blk + 1) * BS)
        wv[LINK0 + blk * NB : LINK0 + (blk + 1) * NB, :] = spread_rows(jnp.concatenate([lw[m0], lw[m1]], axis=1))
        second = lrow[m1] if blk < 2 else jnp.full((1, HALF), -1, jnp.int32)
        hit = row_of == jnp.concatenate([lrow[m0], second], axis=1)
        st[:, lanes] = jnp.where(hit, 1.0, 0.0).astype(BF16)
    bw[0:1, :] = wv[EDGE0 : EDGE0 + 1, :]
    bw[1:8, :] = jnp.broadcast_to(cw[1:2, BS - 1 :], (7, BS))
    upad[0:8, :] = jnp.zeros((8, BS), F32)
    ol_ref[LINKS:, :] = jnp.zeros((64, 2 * BS), F32)
    pl.semaphore_wait(barrier, 2 * (PARTS - 1) + 2)

    sub16 = lax.broadcasted_iota(jnp.int32, (16, BS), 0) % 8

    def products(d, picks):
        lhs = split_rows(d)
        out = jnp.zeros((16, 2 * BS), F32)
        for j, pick in enumerate(picks):
            picked = jnp.where(sub16 == j, lhs, jnp.zeros_like(lhs))
            out = out + jnp.dot(picked, g_ref[pick], preferred_element_type=F32)
        return (out[:8, :BS] + out[8:, BS:]) + (out[:8, BS:] + out[8:, :BS])

    def level_copy(k, li):
        return pltpu.make_async_remote_copy(
            src_ref=send.at[k, li], dst_ref=recv.at[k, li], send_sem=lv_s.at[k, li], recv_sem=lv_r.at[k, li],
            device_id={AXIS: level_partner(me, li)}, device_id_type=MESH)

    def cycle_copy(k, side):
        return pltpu.make_async_remote_copy(
            src_ref=csend.at[k, side], dst_ref=crecv.at[k, side], send_sem=cy_s.at[k, side],
            recv_sem=cy_r.at[k, side], device_id={AXIS: nxt if side == 0 else prv}, device_id_type=MESH)

    def one_copy(k, j):
        return pltpu.make_async_remote_copy(
            src_ref=ar_src.at[k], dst_ref=ar_one.at[k, j], send_sem=a1_s.at[k, j], recv_sem=a1_r.at[k, j],
            device_id={AXIS: one_peer(j)}, device_id_type=MESH)

    def two_copy(k, j):
        return pltpu.make_async_remote_copy(
            src_ref=ar_mid.at[k], dst_ref=ar_two.at[k, j], send_sem=a2_s.at[k, j], recv_sem=a2_r.at[k, j],
            device_id={AXIS: two_peer(j)}, device_id_type=MESH)

    def reduce_begin(k):
        @pl.loop(1, PARTS)
        def _(j):
            one_copy(k, j).start()

    def reduce_middle(k):
        @pl.loop(1, PARTS)
        def _(j):
            one_copy(k, j).wait()

        ar_one[k, 0] = ar_src[k]
        ar_mid[k] = jnp.sum(ar_one[k], axis=0)

        @pl.loop(1, PARTS)
        def _(j):
            two_copy(k, j).start()

    def reduce_end(k):
        @pl.loop(1, PARTS)
        def _(j):
            two_copy(k, j).wait()

        ar_two[k, 0] = ar_mid[k]
        return jnp.sum(ar_two[k], axis=0)

    def put_sums(k, pairs):
        count = -(-len(pairs) // 8) * 8
        parts = [jnp.sum(a * b, axis=0, keepdims=True) for a, b in pairs]
        parts += [jnp.zeros((1, BS), F32)] * (count - len(pairs))
        sums = jnp.sum(jnp.concatenate(parts, axis=0), axis=1, keepdims=True)
        shape = (count, BS)
        own = lax.broadcasted_iota(jnp.int32, shape, 0) == lax.broadcasted_iota(jnp.int32, shape, 1)
        ar_src[k] = jnp.sum(jnp.where(own, jnp.broadcast_to(sums, shape), 0.0), axis=0, keepdims=True)

    def lane(total, i):
        return jnp.broadcast_to(total[:, i : i + 1], (8, BS))

    def wide(value):
        return jnp.tile(value, (NB // 8, 1))

    def convert():
        @pl.loop(0, 16)
        def _(c):
            dict_copy(c).wait()

            @pl.loop(0, 2)
            def _(i):
                for j in range(4):
                    at = c * 8 + i * 4 + j
                    block = stage[at]
                    high = block.astype(BF16)
                    g_ref[at, :, 0:BS] = high
                    g_ref[at, :, BS:] = (block - high.astype(F32)).astype(BF16)

    def operate(k):
        @pl.loop(0, LEVELS)
        def _(i):
            li = LEVELS - 1 - i
            m = level_index(li)

            @pl.loop(0, HALF // 16)
            def _(h):
                for j in range(16):
                    row = rows[m, 0, h * 16 + j]
                    send[k, li, pl.ds(h * 16 + j, 1), :] = upad[pl.ds(row + 8, 1), :]

            level_copy(k, li).start()

        csend[k, 0] = upad[7 + NB : 8 + NB, :]
        csend[k, 1] = upad[8:9, :]
        cycle_copy(k, 0).start()
        cycle_copy(k, 1).start()

        @pl.when(k == 0)
        def _():
            convert()

        def local(t, carry):
            for part in range(4):
                g = pl.multiple_of(t * 32 + part * 8, 8)
                here = upad[pl.ds(g + 8, 8), :]
                before = upad[pl.ds(g + 7, 8), :]
                own = products(here * wv[pl.ds(g, 8), :], [dids[g + j] for j in range(8)])
                acc_ref[pl.ds(g, 8), :] = shift_ref[pl.ds(g, 8), :] * here + own
                edge = (here - before) * wv[pl.ds(EDGE0 + g, 8), :]
                f_ref[pl.ds(g, 8), :] = products(edge, [cids[0, g + j] for j in range(8)])
            return carry

        lax.fori_loop(0, 4, local, 0)

        def level(li, carry):
            level_copy(k, li).wait_recv()
            m = level_index(li)
            for h in range(8):
                c = pl.multiple_of(li * HALF + h * 8, 8)
                diff = send[k, li, h * 8 : h * 8 + 8, :] - recv[k, li, h * 8 : h * 8 + 8, :]
                out = products(diff * wv[pl.ds(LINK0 + c, 8), :], [lids[m, 0, h * 8 + j] for j in range(8)])
                high = out.astype(BF16).astype(F32)
                ol_ref[pl.ds(c, 8), 0:BS] = high
                ol_ref[pl.ds(c, 8), BS:] = out - high
            return carry

        lax.fori_loop(0, LEVELS, level, 0)
        cycle_copy(k, 0).wait()
        cycle_copy(k, 1).wait()
        sub8 = lax.broadcasted_iota(jnp.int32, (8, BS), 0)
        edge = jnp.where(sub8 == 0, upad[8:9, :] - crecv[k, 0], crecv[k, 1] - upad[7 + NB : 8 + NB, :])
        bound = products(edge * bw[...], [cids[0, 0], cids[1, NB - 1]])
        f_ref[0:1, :] = bound[0:1, :]
        f_ref[NB : NB + 1, :] = bound[1:2, :]
        spread = jnp.dot(st[...], ol_ref[...].astype(BF16), preferred_element_type=F32)
        acc_ref[...] = acc_ref[...] + (f_ref[0:NB, :] - f_ref[1 : NB + 1, :]) + (spread[:, :BS] + spread[:, BS:])

        @pl.loop(0, LEVELS)
        def _(li):
            level_copy(k, li).wait_send()

    vecs[0] = upad[8 : 8 + NB, :]

    def iteration(k, carry):
        operate(k)
        vecs[k + 1] = acc_ref[...]

        @pl.when(k < 2)
        def _():
            vec = upad[8 : 8 + NB, :]
            image = acc_ref[...]
            put_sums(k, [(vec, vec), (vec, image)])
            reduce_begin(k)
            upad[8 : 8 + NB, :] = image

        @pl.when((k == 1) | (k == 2))
        def _():
            reduce_middle(k - 1)

        @pl.when(k == 2)
        def _():
            total = reduce_end(0)
            scal[0] = lane(total, 0)
            scal[1] = lane(total, 1)
            upad[8 : 8 + NB, :] = vecs[2] - wide(scal[0] / scal[1]) * vecs[3]

        return carry

    lax.fori_loop(0, ITERS, iteration, 0)
    total = reduce_end(1)
    m0, m1, m2, m3 = scal[0], scal[1], lane(total, 0), lane(total, 1)
    alpha0 = m0 / m1
    norm1 = m0 - 2.0 * alpha0 * m1 + alpha0 * alpha0 * m2
    product1 = m1 - 2.0 * alpha0 * m2 + alpha0 * alpha0 * m3
    beta1 = norm1 / m0
    alpha1 = norm1 / (product1 - beta1 * norm1 / alpha0)
    al0, al1, be1 = wide(alpha0), wide(alpha1), wide(beta1)
    r1 = vecs[0] - al0 * vecs[1]
    w1 = vecs[1] - al0 * vecs[2]
    n1 = upad[8 : 8 + NB, :]
    p1 = r1 + be1 * vecs[0]
    s1 = w1 + be1 * vecs[1]
    z1 = n1 + be1 * vecs[2]
    x_ref[...] = al0 * vecs[0] + al1 * p1
    r2 = r1 - al1 * s1
    w2 = w1 - al1 * z1
    n2 = n1 - al1 * (vecs[4] + be1 * vecs[3])
    put_sums(2, [(r2, r2), (r2, w2), (w2, w2), (r2, s1), (w2, s1), (s1, s1), (r2, n2), (r2, z1), (w2, n2), (w2, z1),
                 (s1, n2), (s1, z1)])
    vecs[0] = p1
    vecs[1] = s1
    vecs[2] = z1
    r_ref[...] = r2
    vecs[3] = w2
    vecs[4] = n2
    reduce_begin(2)
    reduce_middle(2)
    total = reduce_end(2)
    rr, rw, ww, rs, ws, ss, rn, rz, wn, wz, sn, sz = (lane(total, i) for i in range(12))
    beta2 = rr / norm1
    alpha2 = rr / (rw - beta2 * rr / alpha1)
    c, d = alpha2, alpha2 * beta2
    norm3 = rr + c * c * ww + d * d * ss - 2.0 * (c * rw + d * rs - c * d * ws)
    product3 = rw - c * (rn + ww) - d * (rz + ws) + c * c * wn + c * d * (wz + sn) + d * d * sz
    beta3 = norm3 / rr
    alpha3 = norm3 / (product3 - beta3 * norm3 / alpha2)
    al2, be2, al3, be3 = wide(alpha2), wide(beta2), wide(alpha3), wide(beta3)
    p2 = r_ref[...] + be2 * vecs[0]
    s2 = vecs[3] + be2 * vecs[1]
    r3 = r_ref[...] - al2 * s2
    w3 = vecs[3] - al2 * (vecs[4] + be2 * vecs[2])
    x_ref[...] = x_ref[...] + al2 * p2 + al3 * (r3 + be3 * p2)
    r_ref[...] = r3 - al3 * (w3 + be3 * s2)


def per_device(
    right_side,
    diag_shift,
    dictionary,
    diag_ids,
    diag_gain,
    cycle_ids,
    cycle_weights,
    link_rows,
    link_ids,
    link_weights,
):

    vec = (NB, BS)
    across = (1, 0, 2)
    vmem = pl.BlockSpec(memory_space=pltpu.VMEM)
    args = (
        right_side.reshape(vec), diag_shift.reshape(vec), dictionary, diag_ids, diag_gain.reshape(1, NB),
        cycle_ids.T, cycle_weights.T, jnp.transpose(link_rows, across), jnp.transpose(link_ids, across),
        jnp.transpose(link_weights, across),
    )
    solved, residual = pl.pallas_call(
        kernel,
        out_shape=(jax.ShapeDtypeStruct(vec, F32), jax.ShapeDtypeStruct(vec, F32)),
        in_specs=[pl.BlockSpec(memory_space=pl.ANY)] * len(args),
        out_specs=(vmem, vmem),
        scratch_shapes=[
            pltpu.VMEM((BS, BS, 2 * BS), BF16),
            pltpu.VMEM((BS, BS, BS), F32),
            pltpu.VMEM(vec, F32),
            pltpu.SMEM((NB,), jnp.int32),
            pltpu.SMEM((2, NB), jnp.int32),
            pltpu.SMEM((LEVELS, 1, HALF), jnp.int32),
            pltpu.SMEM((LEVELS, 1, HALF), jnp.int32),
            pltpu.VMEM((1, NB), F32),
            pltpu.VMEM((2, NB), F32),
            pltpu.VMEM((LEVELS, 1, HALF), jnp.int32),
            pltpu.VMEM((LEVELS, 1, HALF), F32),
            pltpu.VMEM((LINK0 + 3 * NB, BS), F32),
            pltpu.VMEM((8, BS), F32),
            pltpu.VMEM((NB, 3 * BS), BF16),
            pltpu.VMEM((NB + 8, BS), F32),
            pltpu.VMEM((ITERS + 1, NB, BS), F32),
            pltpu.VMEM(vec, F32),
            pltpu.VMEM((NB + 8, BS), F32),
            pltpu.VMEM((3 * BS, 2 * BS), F32),
            pltpu.VMEM((2, 8, BS), F32),
            pltpu.VMEM((ITERS, LEVELS, HALF, BS), F32),
            pltpu.VMEM((ITERS, LEVELS, HALF, BS), F32),
            pltpu.VMEM((ITERS, 2, 1, BS), F32),
            pltpu.VMEM((ITERS, 2, 1, BS), F32),
            pltpu.VMEM((SUMS, 1, BS), F32),
            pltpu.VMEM((SUMS, PARTS, 1, BS), F32),
            pltpu.VMEM((SUMS, 1, BS), F32),
            pltpu.VMEM((SUMS, PARTS, 1, BS), F32),
            pltpu.SemaphoreType.DMA((len(args),)),
            pltpu.SemaphoreType.DMA((16,)),
            pltpu.SemaphoreType.DMA((ITERS, LEVELS)),
            pltpu.SemaphoreType.DMA((ITERS, LEVELS)),
            pltpu.SemaphoreType.DMA((ITERS, 2)),
            pltpu.SemaphoreType.DMA((ITERS, 2)),
            pltpu.SemaphoreType.DMA((SUMS, PARTS)),
            pltpu.SemaphoreType.DMA((SUMS, PARTS)),
            pltpu.SemaphoreType.DMA((SUMS, PARTS)),
            pltpu.SemaphoreType.DMA((SUMS, PARTS)),
        ],
        compiler_params=pltpu.CompilerParams(
            collective_id=0, has_side_effects=True, vmem_limit_bytes=58 * 1024 * 1024
        ),
        name="cg",
    )(*args)
    return solved.reshape(-1), residual.reshape(-1)


def solution(mesh):
    placed = (
        P(AXIS),
        P(AXIS),
        P(),
        P(AXIS),
        P(AXIS),
        P(AXIS, None),
        P(AXIS, None),
        P(AXIS, None, None),
        P(AXIS, None, None),
        P(AXIS, None, None),
    )
    return jax.shard_map(
        per_device, mesh=mesh, in_specs=placed, out_specs=(P(AXIS), P(AXIS)), check_vma=False
    )
```

time: 79.6 us -> 62.2 us (0.78)
  local copies, waits for them, and re-layouts: 16.8 us -> 2.95 us
  Pallas kernels: 61.8 us -> 58.5 us
    concatenate x3 -> x0, local copies, waits for them, and re-layouts: 4.14 us -> none  [the longest x2 4.06 us: table(): jnp.concatenate([diag, cycle[:, 0], reordered(link), jnp.zeros((64,), dia...]
    squeeze x5 -> x0, local copies, waits for them, and re-layouts: 3.53 us -> none  [the longest x3 2.17 us: reordered(): return jnp.concatenate([values[0, m] for m in LEVEL_OF])]
    unnamed x8 -> x2, local copies, waits for them, and re-layouts: 6.33 us -> 2.95 us
    pallas_call x1, Pallas kernels: 61.8 us -> 58.5 us  [per_device(): pl.pallas_call(kernel, out_shape=(jax.ShapeDtypeStruct(vec, F32), jax.Sha...]
    slice x2 -> x0, local copies, waits for them, and re-layouts: 2.74 us -> none  [table(): cycle[-1, 1:]]
where the time goes in v2:
time: 62.2 us; the launch traced here: 62.1 us
  Pallas kernels  58.5 us (94%)
  local copies, waits for them, and re-layouts  2.95 us (5%)
  between operations  0.64 us (1%)
    pallas_call x1, Pallas kernels, per_device(): pl.pallas_call(kernel, out_shape=(jax.ShapeDtypeStruct(vec, F32), jax.Sha...  58.5 us
    unnamed x2, local copies, waits for them, and re-layouts  2.95 us

profile of v2, /device:TPU:1, one launch (start us, length us, event | category | flops | bytes accessed | tf_op | source)
XLA Modules:
  0.0 62.1 jit_solution(9092063644643898196)
XLA Ops:
  0.6 58.5 %cg.1 = (f32[128,128]{1,0:T(8,128)}, f32[128,128]{1,0:T(8,128)}) custom-call(f32[128,128]{1,0:T(8,128)} %bitcast.10, f32[128,128]{1,0:T(8,128)} %bitcast.11, f32[128,128,128]{2,1,0:T(8,128)} %dict_hbm.1, s32[128]{0:T(128)} %dids_hbm.1, f32[1,128]{1,0:T(1,128)} %bitcast.19, s32[2,128]{1,0:T(2,128)} %bitcast.17, f32[2,128]{1,0:T(2,128)} %bitcast.18, ...), custom_call_target="tpu_custom_call" | custom-call | tf_op jit(solution)/shard_map/cg/pallas_call | solution.py:358
  59.1 1.5 %copy.14 = f32[16384]{0:T(1024)} copy(f32[16384]{0:T(1024)} %bitcast.13) | data formatting | bytes 131072
  60.6 1.5 %copy.15 = f32[16384]{0:T(1024)} copy(f32[16384]{0:T(1024)} %bitcast.12) | data formatting | bytes 131072

commit v3 on v2

--- a/solution.py
+++ b/solution.py
@@ -44,7 +44,7 @@
 
 def kernel(
     b_hbm, shift_hbm, dict_hbm, dids_hbm, gain_hbm, cids_hbm, cw_hbm, lrow_hbm, lids_hbm, lw_hbm,
-    x_ref, r_ref,
+    out_ref,
     g_ref, stage, shift_ref, dids, cids, rows, lids, gain, cw, lrow, lw,
     wv, bw, st, upad, vecs, acc_ref, f_ref, ol_ref, scal,
     send, recv, csend, crecv, ar_src, ar_one, ar_mid, ar_two,
@@ -144,8 +144,7 @@
             device_id={AXIS: two_peer(j)}, device_id_type=MESH)
 
     def reduce_begin(k):
-        @pl.loop(1, PARTS)
-        def _(j):
+        for j in sorted(range(1, PARTS), key=lambda j: abs(j // 2 - 4)):
             one_copy(k, j).start()
 
     def reduce_middle(k):
@@ -156,8 +155,7 @@
         ar_one[k, 0] = ar_src[k]
         ar_mid[k] = jnp.sum(ar_one[k], axis=0)
 
-        @pl.loop(1, PARTS)
-        def _(j):
+        for j in sorted(range(1, PARTS), key=lambda j: abs(j // 4 - 2) + abs(j % 4 - 2)):
             two_copy(k, j).start()
 
     def reduce_end(k):
@@ -203,11 +201,11 @@
             li = LEVELS - 1 - i
             m = level_index(li)
 
-            @pl.loop(0, HALF // 16)
+            @pl.loop(0, HALF // 32)
             def _(h):
-                for j in range(16):
-                    row = rows[m, 0, h * 16 + j]
-                    send[k, li, pl.ds(h * 16 + j, 1), :] = upad[pl.ds(row + 8, 1), :]
+                found = [upad[pl.ds(rows[m, 0, h * 32 + j] + 8, 1), :] for j in range(32)]
+                for j in range(32):
+                    send[k, li, pl.ds(h * 32 + j, 1), :] = found[j]
 
             level_copy(k, li).start()
 
@@ -221,8 +219,8 @@
             convert()
 
         def local(t, carry):
-            for part in range(4):
-                g = pl.multiple_of(t * 32 + part * 8, 8)
+            for part in range(8):
+                g = pl.multiple_of(t * 64 + part * 8, 8)
                 here = upad[pl.ds(g + 8, 8), :]
                 before = upad[pl.ds(g + 7, 8), :]
                 own = products(here * wv[pl.ds(g, 8), :], [dids[g + j] for j in range(8)])
@@ -231,10 +229,9 @@
                 f_ref[pl.ds(g, 8), :] = products(edge, [cids[0, g + j] for j in range(8)])
             return carry
 
-        lax.fori_loop(0, 4, local, 0)
-
-        def level(li, carry):
-            level_copy(k, li).wait_recv()
+        lax.fori_loop(0, 2, local, 0)
+
+        def level(li):
             m = level_index(li)
             for h in range(8):
                 c = pl.multiple_of(li * HALF + h * 8, 8)
@@ -243,9 +240,17 @@
                 high = out.astype(BF16).astype(F32)
                 ol_ref[pl.ds(c, 8), 0:BS] = high
                 ol_ref[pl.ds(c, 8), BS:] = out - high
+
+        def two_levels(i, carry):
+            level_copy(k, 2 * i).wait_recv()
+            level_copy(k, 2 * i + 1).wait_recv()
+            level(2 * i)
+            level(2 * i + 1)
             return carry
 
-        lax.fori_loop(0, LEVELS, level, 0)
+        lax.fori_loop(0, LEVELS // 2, two_levels, 0)
+        level_copy(k, LEVELS - 1).wait_recv()
+        level(LEVELS - 1)
         cycle_copy(k, 0).wait()
         cycle_copy(k, 1).wait()
         sub8 = lax.broadcasted_iota(jnp.int32, (8, BS), 0)
@@ -302,7 +307,7 @@
     p1 = r1 + be1 * vecs[0]
     s1 = w1 + be1 * vecs[1]
     z1 = n1 + be1 * vecs[2]
-    x_ref[...] = al0 * vecs[0] + al1 * p1
+    out_ref[0] = al0 * vecs[0] + al1 * p1
     r2 = r1 - al1 * s1
     w2 = w1 - al1 * z1
     n2 = n1 - al1 * (vecs[4] + be1 * vecs[3])
@@ -311,7 +316,7 @@
     vecs[0] = p1
     vecs[1] = s1
     vecs[2] = z1
-    r_ref[...] = r2
+    out_ref[1] = r2
     vecs[3] = w2
     vecs[4] = n2
     reduce_begin(2)
@@ -326,12 +331,12 @@
     beta3 = norm3 / rr
     alpha3 = norm3 / (product3 - beta3 * norm3 / alpha2)
     al2, be2, al3, be3 = wide(alpha2), wide(beta2), wide(alpha3), wide(beta3)
-    p2 = r_ref[...] + be2 * vecs[0]
+    p2 = out_ref[1] + be2 * vecs[0]
     s2 = vecs[3] + be2 * vecs[1]
-    r3 = r_ref[...] - al2 * s2
+    r3 = out_ref[1] - al2 * s2
     w3 = vecs[3] - al2 * (vecs[4] + be2 * vecs[2])
-    x_ref[...] = x_ref[...] + al2 * p2 + al3 * (r3 + be3 * p2)
-    r_ref[...] = r3 - al3 * (w3 + be3 * s2)
+    out_ref[0] = out_ref[0] + al2 * p2 + al3 * (r3 + be3 * p2)
+    out_ref[1] = r3 - al3 * (w3 + be3 * s2)
 
 
 def per_device(
@@ -355,11 +360,11 @@
         cycle_ids.T, cycle_weights.T, jnp.transpose(link_rows, across), jnp.transpose(link_ids, across),
         jnp.transpose(link_weights, across),
     )
-    solved, residual = pl.pallas_call(
+    out = pl.pallas_call(
         kernel,
-        out_shape=(jax.ShapeDtypeStruct(vec, F32), jax.ShapeDtypeStruct(vec, F32)),
+        out_shape=jax.ShapeDtypeStruct((2, *vec), F32),
         in_specs=[pl.BlockSpec(memory_space=pl.ANY)] * len(args),
-        out_specs=(vmem, vmem),
+        out_specs=vmem,
         scratch_shapes=[
             pltpu.VMEM((BS, BS, 2 * BS), BF16),
             pltpu.VMEM((BS, BS, BS), F32),
@@ -405,7 +410,7 @@
         ),
         name="cg",
     )(*args)
-    return solved.reshape(-1), residual.reshape(-1)
+    return out[0].reshape(-1), out[1].reshape(-1)
 
 
 def solution(mesh):

time: 62.2 us -> 57.9 us (0.931)
  Pallas kernels: 58.5 us -> 55.6 us
  local copies, waits for them, and re-layouts: 2.95 us -> 1.53 us
    unnamed x2 -> x0, local copies, waits for them, and re-layouts: 2.95 us -> none
    pallas_call x1, Pallas kernels: 58.5 us -> 55.6 us  [per_device(): pl.pallas_call(kernel, out_shape=jax.ShapeDtypeStruct((2, *vec), F32), in...]
    another operation x0 -> x1, local copies, waits for them, and re-layouts: none -> 1.53 us  [per_device(): return (out[0].reshape(-1), out[1].reshape(-1))]
where the time goes in v3:
time: 57.9 us; the launch traced here: 57.8 us
  Pallas kernels  55.6 us (96%)
  local copies, waits for them, and re-layouts  1.53 us (3%)
  between operations  0.64 us (1%)
    pallas_call x1, Pallas kernels, per_device(): pl.pallas_call(kernel, out_shape=jax.ShapeDtypeStruct((2, *vec), F32), in...  55.6 us
    another operation x1, local copies, waits for them, and re-layouts, per_device(): return (out[0].reshape(-1), out[1].reshape(-1))  1.53 us

profile of v3, /device:TPU:1, one launch (start us, length us, event | category | flops | bytes accessed | tf_op | source)
XLA Modules:
  0.0 57.8 jit_solution(16663548857736404836)
XLA Ops:
  0.6 55.6 %cg.1 = f32[2,128,128]{2,1,0:T(8,128)} custom-call(f32[128,128]{1,0:T(8,128)} %bitcast.12, f32[128,128]{1,0:T(8,128)} %bitcast.13, f32[128,128,128]{2,1,0:T(8,128)} %dict_hbm.1, s32[128]{0:T(128)} %dids_hbm.1, f32[1,128]{1,0:T(1,128)} %bitcast.19, s32[2,128]{1,0:T(2,128)} %bitcast.17, f32[2,128]{1,0:T(2,128)} %bitcast.18, s32[5,1,64]{2,1,0:T(1,128)} %bitcast.14, ...), custom_call_target="tpu_custom_call" | custom-call | tf_op jit(solution)/shard_map/cg/pallas_call | solution.py:363
  56.3 1.5 %slice_bitcast_fusion = (f32[16384]{0:T(1024)}, f32[16384]{0:T(1024)}) fusion(f32[2,128,128]{2,1,0:T(8,128)} %cg.1), kind=kLoop, calls=%fused_computation | loop fusion | bytes 262144 | tf_op jit(solution)/shard_map/reshape;squeeze | solution.py:413

commit v4 on v3

--- a/solution.py
+++ b/solution.py
@@ -46,7 +46,7 @@
     b_hbm, shift_hbm, dict_hbm, dids_hbm, gain_hbm, cids_hbm, cw_hbm, lrow_hbm, lids_hbm, lw_hbm,
     out_ref,
     g_ref, stage, shift_ref, dids, cids, rows, lids, gain, cw, lrow, lw,
-    wv, bw, st, upad, vecs, acc_ref, f_ref, ol_ref, scal,
+    wv, bw, st, upad, vecs, acc_ref, f_ref, ol_ref, scal, kept, part_sums,
     send, recv, csend, crecv, ar_src, ar_one, ar_mid, ar_two,
     in_sem, dict_sem, lv_s, lv_r, cy_s, cy_r, a1_s, a1_r, a2_s, a2_r,
 ):
@@ -148,28 +148,28 @@
             one_copy(k, j).start()
 
     def reduce_middle(k):
-        @pl.loop(1, PARTS)
-        def _(j):
-            one_copy(k, j).wait()
-
+        for j in range(1, PARTS):
+            one_copy(k, j).wait_recv()
         ar_one[k, 0] = ar_src[k]
         ar_mid[k] = jnp.sum(ar_one[k], axis=0)
 
         for j in sorted(range(1, PARTS), key=lambda j: abs(j // 4 - 2) + abs(j % 4 - 2)):
             two_copy(k, j).start()
+        for j in range(1, PARTS):
+            one_copy(k, j).wait_send()
 
     def reduce_end(k):
-        @pl.loop(1, PARTS)
-        def _(j):
+        for j in range(1, PARTS):
             two_copy(k, j).wait()
-
         ar_two[k, 0] = ar_mid[k]
         return jnp.sum(ar_two[k], axis=0)
 
-    def put_sums(k, pairs):
-        count = -(-len(pairs) // 8) * 8
-        parts = [jnp.sum(a * b, axis=0, keepdims=True) for a, b in pairs]
-        parts += [jnp.zeros((1, BS), F32)] * (count - len(pairs))
+    def row_sums(a, b):
+        return jnp.sum(a * b, axis=0, keepdims=True)
+
+    def put_sums(k, parts):
+        count = -(-len(parts) // 8) * 8
+        parts = parts + [jnp.zeros((1, BS), F32)] * (count - len(parts))
         sums = jnp.sum(jnp.concatenate(parts, axis=0), axis=1, keepdims=True)
         shape = (count, BS)
         own = lax.broadcasted_iota(jnp.int32, shape, 0) == lax.broadcasted_iota(jnp.int32, shape, 1)
@@ -195,6 +195,33 @@
                     g_ref[at, :, 0:BS] = high
                     g_ref[at, :, BS:] = (block - high.astype(F32)).astype(BF16)
 
+    def prepare():
+        total = reduce_end(1)
+        m0, m1, m2, m3 = scal[0], scal[1], lane(total, 0), lane(total, 1)
+        alpha0 = m0 / m1
+        norm1 = m0 - 2.0 * alpha0 * m1 + alpha0 * alpha0 * m2
+        product1 = m1 - 2.0 * alpha0 * m2 + alpha0 * alpha0 * m3
+        beta1 = norm1 / m0
+        alpha1 = norm1 / (product1 - beta1 * norm1 / alpha0)
+        scal[2] = norm1
+        scal[3] = alpha1
+        al0, al1, be1 = wide(alpha0), wide(alpha1), wide(beta1)
+        r1 = vecs[0] - al0 * vecs[1]
+        w1 = vecs[1] - al0 * vecs[2]
+        n1 = upad[8 : 8 + NB, :]
+        p1 = r1 + be1 * vecs[0]
+        s1 = w1 + be1 * vecs[1]
+        z1 = n1 + be1 * vecs[2]
+        out_ref[0] = al0 * vecs[0] + al1 * p1
+        r2 = r1 - al1 * s1
+        w2 = w1 - al1 * z1
+        for i, value in enumerate((p1, s1, z1, r2, w2, n1 - al1 * (be1 * vecs[3]))):
+            kept[i] = value
+        for i, (a, b) in enumerate(
+            ((r2, r2), (r2, w2), (w2, w2), (r2, s1), (w2, s1), (s1, s1), (r2, z1), (w2, z1), (s1, z1))
+        ):
+            part_sums[i : i + 1, :] = row_sums(a, b)
+
     def operate(k):
         @pl.loop(0, LEVELS)
         def _(i):
@@ -217,6 +244,16 @@
         @pl.when(k == 0)
         def _():
             convert()
+
+        @pl.when(k >= 2)
+        def _():
+            reduce_middle(k - 2)
+
+        @pl.when((k == 1) | (k == 2))
+        def _():
+            vec = vecs[k - 1]
+            put_sums(k - 1, [row_sums(vec, vec), row_sums(vec, vecs[k])])
+            reduce_begin(k - 1)
 
         def local(t, carry):
             for part in range(8):
@@ -249,6 +286,17 @@
             return carry
 
         lax.fori_loop(0, LEVELS // 2, two_levels, 0)
+
+        @pl.when(k == 2)
+        def _():
+            total = reduce_end(0)
+            scal[0] = lane(total, 0)
+            scal[1] = lane(total, 1)
+
+        @pl.when(k == 3)
+        def _():
+            prepare()
+
         level_copy(k, LEVELS - 1).wait_recv()
         level(LEVELS - 1)
         cycle_copy(k, 0).wait()
@@ -261,8 +309,7 @@
         spread = jnp.dot(st[...], ol_ref[...].astype(BF16), preferred_element_type=F32)
         acc_ref[...] = acc_ref[...] + (f_ref[0:NB, :] - f_ref[1 : NB + 1, :]) + (spread[:, :BS] + spread[:, BS:])
 
-        @pl.loop(0, LEVELS)
-        def _(li):
+        for li in range(LEVELS):
             level_copy(k, li).wait_send()
 
     vecs[0] = upad[8 : 8 + NB, :]
@@ -273,56 +320,24 @@
 
         @pl.when(k < 2)
         def _():
-            vec = upad[8 : 8 + NB, :]
-            image = acc_ref[...]
-            put_sums(k, [(vec, vec), (vec, image)])
-            reduce_begin(k)
-            upad[8 : 8 + NB, :] = image
-
-        @pl.when((k == 1) | (k == 2))
-        def _():
-            reduce_middle(k - 1)
+            upad[8 : 8 + NB, :] = acc_ref[...]
 
         @pl.when(k == 2)
         def _():
-            total = reduce_end(0)
-            scal[0] = lane(total, 0)
-            scal[1] = lane(total, 1)
             upad[8 : 8 + NB, :] = vecs[2] - wide(scal[0] / scal[1]) * vecs[3]
 
         return carry
 
     lax.fori_loop(0, ITERS, iteration, 0)
-    total = reduce_end(1)
-    m0, m1, m2, m3 = scal[0], scal[1], lane(total, 0), lane(total, 1)
-    alpha0 = m0 / m1
-    norm1 = m0 - 2.0 * alpha0 * m1 + alpha0 * alpha0 * m2
-    product1 = m1 - 2.0 * alpha0 * m2 + alpha0 * alpha0 * m3
-    beta1 = norm1 / m0
-    alpha1 = norm1 / (product1 - beta1 * norm1 / alpha0)
-    al0, al1, be1 = wide(alpha0), wide(alpha1), wide(beta1)
-    r1 = vecs[0] - al0 * vecs[1]
-    w1 = vecs[1] - al0 * vecs[2]
-    n1 = upad[8 : 8 + NB, :]
-    p1 = r1 + be1 * vecs[0]
-    s1 = w1 + be1 * vecs[1]
-    z1 = n1 + be1 * vecs[2]
-    out_ref[0] = al0 * vecs[0] + al1 * p1
-    r2 = r1 - al1 * s1
-    w2 = w1 - al1 * z1
-    n2 = n1 - al1 * (vecs[4] + be1 * vecs[3])
-    put_sums(2, [(r2, r2), (r2, w2), (w2, w2), (r2, s1), (w2, s1), (s1, s1), (r2, n2), (r2, z1), (w2, n2), (w2, z1),
-                 (s1, n2), (s1, z1)])
-    vecs[0] = p1
-    vecs[1] = s1
-    vecs[2] = z1
-    out_ref[1] = r2
-    vecs[3] = w2
-    vecs[4] = n2
+    norm1, alpha1 = scal[2], scal[3]
+    n2 = kept[5] - wide(alpha1) * acc_ref[...]
+    kept[5] = n2
+    late = [row_sums(kept[3], n2), row_sums(kept[4], n2), row_sums(kept[1], n2)]
+    put_sums(2, [part_sums[i : i + 1, :] for i in range(9)] + late)
     reduce_begin(2)
     reduce_middle(2)
     total = reduce_end(2)
-    rr, rw, ww, rs, ws, ss, rn, rz, wn, wz, sn, sz = (lane(total, i) for i in range(12))
+    rr, rw, ww, rs, ws, ss, rz, wz, sz, rn, wn, sn = (lane(total, i) for i in range(12))
     beta2 = rr / norm1
     alpha2 = rr / (rw - beta2 * rr / alpha1)
     c, d = alpha2, alpha2 * beta2
@@ -331,10 +346,10 @@
     beta3 = norm3 / rr
     alpha3 = norm3 / (product3 - beta3 * norm3 / alpha2)
     al2, be2, al3, be3 = wide(alpha2), wide(beta2), wide(alpha3), wide(beta3)
-    p2 = out_ref[1] + be2 * vecs[0]
-    s2 = vecs[3] + be2 * vecs[1]
-    r3 = out_ref[1] - al2 * s2
-    w3 = vecs[3] - al2 * (vecs[4] + be2 * vecs[2])
+    p2 = kept[3] + be2 * kept[0]
+    s2 = kept[4] + be2 * kept[1]
+    r3 = kept[3] - al2 * s2
+    w3 = kept[4] - al2 * (kept[5] + be2 * kept[2])
     out_ref[0] = out_ref[0] + al2 * p2 + al3 * (r3 + be3 * p2)
     out_ref[1] = r3 - al3 * (w3 + be3 * s2)
 
@@ -385,7 +400,9 @@
             pltpu.VMEM(vec, F32),
             pltpu.VMEM((NB + 8, BS), F32),
             pltpu.VMEM((3 * BS, 2 * BS), F32),
-            pltpu.VMEM((2, 8, BS), F32),
+            pltpu.VMEM((4, 8, BS), F32),
+            pltpu.VMEM((6, NB, BS), F32),
+            pltpu.VMEM((16, BS), F32),
             pltpu.VMEM((ITERS, LEVELS, HALF, BS), F32),
             pltpu.VMEM((ITERS, LEVELS, HALF, BS), F32),
             pltpu.VMEM((ITERS, 2, 1, BS), F32),

time: 57.9 us -> 56.9 us (0.983)
  Pallas kernels: 55.6 us -> 54.6 us
    pallas_call x1, Pallas kernels: 55.6 us -> 54.6 us  [per_device(): pl.pallas_call(kernel, out_shape=jax.ShapeDtypeStruct((2, *vec), F32), in...]
where the time goes in v4:
time: 56.9 us; the launch traced here: 56.7 us
  Pallas kernels  54.6 us (96%)
  local copies, waits for them, and re-layouts  1.53 us (3%)
  between operations  0.64 us (1%)
    pallas_call x1, Pallas kernels, per_device(): pl.pallas_call(kernel, out_shape=jax.ShapeDtypeStruct((2, *vec), F32), in...  54.6 us
    another operation x1, local copies, waits for them, and re-layouts, per_device(): return (out[0].reshape(-1), out[1].reshape(-1))  1.53 us

profile of v4, /device:TPU:1, one launch (start us, length us, event | category | flops | bytes accessed | tf_op | source)
XLA Modules:
  0.0 56.7 jit_solution(14288764937449331629)
XLA Ops:
  0.6 54.6 %cg.1 = f32[2,128,128]{2,1,0:T(8,128)} custom-call(f32[128,128]{1,0:T(8,128)} %bitcast.12, f32[128,128]{1,0:T(8,128)} %bitcast.13, f32[128,128,128]{2,1,0:T(8,128)} %dict_hbm.1, s32[128]{0:T(128)} %dids_hbm.1, f32[1,128]{1,0:T(1,128)} %bitcast.19, s32[2,128]{1,0:T(2,128)} %bitcast.17, f32[2,128]{1,0:T(2,128)} %bitcast.18, s32[5,1,64]{2,1,0:T(1,128)} %bitcast.14, ...), custom_call_target="tpu_custom_call" | custom-call | tf_op jit(solution)/shard_map/cg/pallas_call | solution.py:378
  55.2 1.5 %slice_bitcast_fusion = (f32[16384]{0:T(1024)}, f32[16384]{0:T(1024)}) fusion(f32[2,128,128]{2,1,0:T(8,128)} %cg.1), kind=kLoop, calls=%fused_computation | loop fusion | bytes 262144 | tf_op jit(solution)/shard_map/reshape;squeeze | solution.py:430

commit v5 on v4

--- a/solution.py
+++ b/solution.py
@@ -223,13 +223,9 @@
             part_sums[i : i + 1, :] = row_sums(a, b)
 
     def operate(k):
-        @pl.loop(0, LEVELS)
-        def _(i):
-            li = LEVELS - 1 - i
+        for li in reversed(range(LEVELS)):
             m = level_index(li)
-
-            @pl.loop(0, HALF // 32)
-            def _(h):
+            for h in range(HALF // 32):
                 found = [upad[pl.ds(rows[m, 0, h * 32 + j] + 8, 1), :] for j in range(32)]
                 for j in range(32):
                     send[k, li, pl.ds(h * 32 + j, 1), :] = found[j]

time: 56.9 us -> 55.3 us (0.972)
  Pallas kernels: 54.6 us -> 53 us
    pallas_call x1, Pallas kernels: 54.6 us -> 53 us  [per_device(): pl.pallas_call(kernel, out_shape=jax.ShapeDtypeStruct((2, *vec), F32), in...]
where the time goes in v5:
time: 55.3 us; the launch traced here: 55.2 us
  Pallas kernels  53 us (96%)
  local copies, waits for them, and re-layouts  1.53 us (3%)
  between operations  0.64 us (1%)
    pallas_call x1, Pallas kernels, per_device(): pl.pallas_call(kernel, out_shape=jax.ShapeDtypeStruct((2, *vec), F32), in...  53 us
    another operation x1, local copies, waits for them, and re-layouts, per_device(): return (out[0].reshape(-1), out[1].reshape(-1))  1.53 us

profile of v5, /device:TPU:1, one launch (start us, length us, event | category | flops | bytes accessed | tf_op | source)
XLA Modules:
  0.0 55.2 jit_solution(9150720331202986863)
XLA Ops:
  0.6 53.0 %cg.1 = f32[2,128,128]{2,1,0:T(8,128)} custom-call(f32[128,128]{1,0:T(8,128)} %bitcast.12, f32[128,128]{1,0:T(8,128)} %bitcast.13, f32[128,128,128]{2,1,0:T(8,128)} %dict_hbm.1, s32[128]{0:T(128)} %dids_hbm.1, f32[1,128]{1,0:T(1,128)} %bitcast.19, s32[2,128]{1,0:T(2,128)} %bitcast.17, f32[2,128]{1,0:T(2,128)} %bitcast.18, s32[5,1,64]{2,1,0:T(1,128)} %bitcast.14, ...), custom_call_target="tpu_custom_call" | custom-call | tf_op jit(solution)/shard_map/cg/pallas_call | solution.py:374
  53.7 1.5 %slice_bitcast_fusion = (f32[16384]{0:T(1024)}, f32[16384]{0:T(1024)}) fusion(f32[2,128,128]{2,1,0:T(8,128)} %cg.1), kind=kLoop, calls=%fused_computation | loop fusion | bytes 262144 | tf_op jit(solution)/shard_map/reshape;squeeze | solution.py:426
